TPU v7x, 32 devices: a whole 2x2x4 slice. The times are simulated.
32 devices in a mesh: dp: 16 (over z, x, core), tensor: 2 (over y).
Axes of the slice: x: 2, y: 2, z: 4, core: 2. Of those that a mesh axis runs over, the one named last changes fastest.
Arguments:
- inputs: float32 [8192, 1024], P('dp'), may hold values from -6 to 6
- ln1_gain: float32 [1024], replicated, may hold values from 0.1 to 1.9
- ln1_bias: float32 [1024], replicated, may hold values from -2.5 to 2.5
- w_query: bfloat16 [1024, 1024], P(None, 'tensor'), may hold values from -0.1875 to 0.1875
- w_key: bfloat16 [1024, 1024], P(None, 'tensor'), may hold values from -0.1875 to 0.1875
- w_value: bfloat16 [1024, 1024], P(None, 'tensor'), may hold values from -0.1875 to 0.1875
- w_out: bfloat16 [1024, 1024], P('tensor'), may hold values from -6 to 6
- ln2_gain: float32 [1024], replicated, may hold values from 0.1 to 1.9
- ln2_bias: float32 [1024], replicated, may hold values from -2.5 to 2.5
- w_up: bfloat16 [1024, 4096], P(None, 'tensor'), may hold values from -0.1875 to 0.1875
- w_down: bfloat16 [4096, 1024], P('tensor'), may hold values from -0.09375 to 0.09375
- teacher: float32 [8192, 1024], P('dp'), may hold values from -5 to 5
- valid_mask: int32 [8192], P('dp'), may hold values from 0 to 1, as said below
Outputs:
- output: float32 [8192, 1024], P('dp')
- loss_value: float32 [], replicated
- input_grad: float32 [8192, 1024], P('dp')
- grad_ln1_gain: float32 [1024], P('dp')
- grad_ln1_bias: float32 [1024], P('dp')
- grad_query: float32 [1024, 1024], P('dp', 'tensor')
- grad_key: float32 [1024, 1024], P('dp', 'tensor')
- grad_value: float32 [1024, 1024], P('dp', 'tensor')
- grad_out: float32 [1024, 1024], P('tensor', 'dp')
- grad_ln2_gain: float32 [1024], P('dp')
- grad_ln2_bias: float32 [1024], P('dp')
- grad_up: float32 [1024, 4096], P('dp', 'tensor')
- grad_down: float32 [4096, 1024], P('tensor', 'dp')
Inputs may be any that keep to these rules, and one draw needn't show every extreme that they name: `valid_mask`: the first token of each block of 512 rows is valid.
All inputs are finite; a program needn't handle non-finite values.
Results may differ from a plain program's by a relative error of at most 0.015.
Values may be sent and summed in bfloat16 or wider, within the bound.
A program may use at most 192 MiB of HBM per device.

v0:
```python
import jax
import jax.numpy as jnp
from jax import lax
from jax.sharding import PartitionSpec as P

HEAD_DIM = 128
SEQ_DEV = 16


EPSILON = 1e-05
NEGATIVE = -1e30


def shifted(value, axis, steps):
    count = lax.axis_size(axis)
    leading, last = (max(0, -steps), min(count, count - steps))
    return lax.ppermute(value, axis, [(source, source + steps) for source in range(leading, last)])


def shifted_2(value, axis, steps):
    count = lax.axis_size(axis)
    pairs = [(source, (source + steps) % count) for source in range(count)]
    return lax.ppermute(value, axis, pairs)


def norm_forward(values, gain_vec, bias_vec):
    average = jnp.mean(values, axis=-1, keepdims=True)
    centred = values - average
    inverse = lax.rsqrt(jnp.mean(centred * centred, axis=-1, keepdims=True) + EPSILON)
    normed = centred * inverse
    return ((normed * gain_vec + bias_vec).astype(jnp.bfloat16), normed, inverse)


def norm_backward(grad_in, normed, inverse, gain_vec):
    scaled = grad_in * gain_vec
    first_mean = jnp.mean(scaled, axis=-1, keepdims=True)
    second_mean = jnp.mean(scaled * normed, axis=-1, keepdims=True)
    result = inverse * (scaled - first_mean - normed * second_mean)
    return (result, jnp.sum(grad_in * normed, axis=0), jnp.sum(grad_in, axis=0))


def contract_rows(left, right):
    return lax.dot_general(
        left, right, (((0,), (0,)), ((), ())), preferred_element_type=jnp.float32
    )


def contract_cols(left, right):
    return lax.dot_general(
        left, right, (((1,), (1,)), ((), ())), preferred_element_type=jnp.float32
    )


def head_scores(queries, keys_now, allowed):
    raw_scores = jnp.einsum(
        "qhe,khe->hqk", queries, keys_now, preferred_element_type=jnp.float32
    ) * HEAD_DIM ** (-0.5)
    return jnp.where(allowed, raw_scores, NEGATIVE)


def stat_add(queries, keys_now, allowed, run_max, run_sum):
    scores = head_scores(queries, keys_now, allowed)
    new_max = jnp.maximum(run_max, jnp.max(scores, axis=-1))
    new_sum = run_sum * jnp.exp(run_max - new_max) + jnp.sum(
        jnp.exp(scores - new_max[..., None]), axis=-1
    )
    return (new_max, new_sum)


def value_add(queries, keys_now, values_now, allowed, log_total, running):
    scores = head_scores(queries, keys_now, allowed)
    prob_rows = jnp.exp(scores - log_total[..., None]).astype(jnp.bfloat16)
    return running + jnp.einsum(
        "hqk,khe->qhe", prob_rows, values_now, preferred_element_type=jnp.float32
    )


def grad_terms(queries, keys_now, values_now, allowed, log_total, d_context, delta_row):
    head_scale = HEAD_DIM ** (-0.5)
    scores = head_scores(queries, keys_now, allowed)
    prob_rows = jnp.exp(scores - log_total[..., None])
    d_probs = jnp.einsum("qhe,khe->hqk", d_context, values_now, preferred_element_type=jnp.float32)
    d_scores = (prob_rows * (d_probs - delta_row[..., None])).astype(jnp.bfloat16)
    d_query = (
        jnp.einsum("hqk,khe->qhe", d_scores, keys_now, preferred_element_type=jnp.float32)
        * head_scale
    )
    d_key = (
        jnp.einsum("hqk,qhe->khe", d_scores, queries, preferred_element_type=jnp.float32)
        * head_scale
    )
    d_value = jnp.einsum(
        "hqk,qhe->khe",
        prob_rows.astype(jnp.bfloat16),
        d_context,
        preferred_element_type=jnp.float32,
    )
    return (d_query, d_key, d_value)


def per_device(
    inputs,
    ln1_gain,
    ln1_bias,
    w_query,
    w_key,
    w_value,
    w_out,
    ln2_gain,
    ln2_bias,
    w_up,
    w_down,
    teacher,
    valid_mask,
):
    row_count = inputs.shape[0]
    local_heads = w_query.shape[1] // HEAD_DIM
    group_pos = lax.axis_index("dp") % SEQ_DEV
    causal = lax.broadcasted_iota(jnp.int32, (row_count, row_count), 0) >= lax.broadcasted_iota(
        jnp.int32, (row_count, row_count), 1
    )
    n_one, normed_one, inverse_one = norm_forward(inputs, ln1_gain, ln1_bias)

    def project(weight):
        return (
            jnp.dot(n_one, weight, preferred_element_type=jnp.float32)
            .astype(jnp.bfloat16)
            .reshape(row_count, local_heads, HEAD_DIM)
        )

    queries = project(w_query)
    keys_own = project(w_key)
    values_own = project(w_value)
    start_max = jnp.full((local_heads, row_count), NEGATIVE, jnp.float32)
    start_sum = jnp.zeros((local_heads, row_count), jnp.float32)
    first_max, first_sum = stat_add(queries, keys_own, causal, start_max, start_sum)
    zero_heads = jnp.zeros((row_count, local_heads, HEAD_DIM), jnp.float32)
    store_shape = (SEQ_DEV, row_count, local_heads, HEAD_DIM)
    key_start = lax.dynamic_update_index_in_dim(
        jnp.zeros(store_shape, jnp.bfloat16), keys_own, 0, 0
    )
    value_start = lax.dynamic_update_index_in_dim(
        jnp.zeros(store_shape, jnp.bfloat16), values_own, 0, 0
    )

    def keep_step(hop_index, state_now):
        keys_now, values_now, key_store, value_store = state_now
        keys_now, values_now = shifted((keys_now, values_now), "dp", 1)
        key_store = lax.dynamic_update_index_in_dim(key_store, keys_now, hop_index, 0)
        value_store = lax.dynamic_update_index_in_dim(value_store, values_now, hop_index, 0)
        return (keys_now, values_now, key_store, value_store)

    kept_state = lax.fori_loop(
        1, SEQ_DEV, keep_step, (keys_own, values_own, key_start, value_start)
    )
    key_store = kept_state[2]
    value_store = kept_state[3]

    def fetch(hop_index):
        stored_keys = lax.dynamic_index_in_dim(key_store, hop_index, 0, keepdims=False)
        stored_values = lax.dynamic_index_in_dim(value_store, hop_index, 0, keepdims=False)
        return (stored_keys, stored_values)

    def stat_step(hop_index, state_now):
        stored_keys, unused_values = fetch(hop_index)
        return stat_add(queries, stored_keys, hop_index <= group_pos, state_now[0], state_now[1])

    run_max, run_sum = lax.fori_loop(1, SEQ_DEV, stat_step, (first_max, first_sum))
    log_total = run_max + jnp.log(run_sum)

    def value_step(hop_index, running):
        stored_keys, stored_values = fetch(hop_index)
        return value_add(
            queries, stored_keys, stored_values, hop_index <= group_pos, log_total, running
        )

    first_out = value_add(queries, keys_own, values_own, causal, log_total, zero_heads)
    attn = lax.fori_loop(1, SEQ_DEV, value_step, first_out)
    context = attn.astype(jnp.bfloat16).reshape(row_count, local_heads * HEAD_DIM)
    hidden = inputs + lax.psum(
        jnp.dot(context, w_out, preferred_element_type=jnp.float32).astype(jnp.bfloat16), "tensor"
    ).astype(jnp.float32)
    n_two, normed_two, inverse_two = norm_forward(hidden, ln2_gain, ln2_bias)
    pre_act = jnp.dot(n_two, w_up, preferred_element_type=jnp.float32)
    active = jnp.maximum(pre_act, 0.0).astype(jnp.bfloat16)
    output = hidden + lax.psum(
        jnp.dot(active, w_down, preferred_element_type=jnp.float32).astype(jnp.bfloat16), "tensor"
    ).astype(jnp.float32)
    weight_rows = valid_mask.astype(jnp.float32)
    misfit = output - teacher
    error_total, valid_total = lax.psum(
        (jnp.sum(weight_rows[:, None] * misfit * misfit), jnp.sum(weight_rows)), "dp"
    )
    loss_value = error_total / (2.0 * valid_total)
    token_total = row_count * lax.axis_size("dp")
    d_output = token_total / valid_total * weight_rows[:, None] * misfit
    g_ffn = d_output.astype(jnp.bfloat16)
    grad_down = contract_rows(active, g_ffn)
    d_active = contract_cols(g_ffn, w_down)
    d_pre = jnp.where(pre_act > 0.0, d_active, 0.0).astype(jnp.bfloat16)
    grad_up = contract_rows(n_two, d_pre)
    d_n_two = lax.psum(contract_cols(d_pre, w_up).astype(jnp.bfloat16), "tensor").astype(
        jnp.float32
    )
    d_hidden_norm, grad_ln2_gain, grad_ln2_bias = norm_backward(
        d_n_two, normed_two, inverse_two, ln2_gain
    )
    d_hidden = d_output + d_hidden_norm
    g_attn = d_hidden.astype(jnp.bfloat16)
    grad_out = contract_rows(context, g_attn)
    d_context = (
        contract_cols(g_attn, w_out).astype(jnp.bfloat16).reshape(row_count, local_heads, HEAD_DIM)
    )
    delta_row = jnp.einsum("qhe,qhe->hq", d_context.astype(jnp.float32), attn)
    own_query, own_key, own_value = grad_terms(
        queries, keys_own, values_own, causal, log_total, d_context, delta_row
    )

    def back_step(hop_index, state_now):
        keys_now, values_now, key_acc, value_acc, query_acc = state_now
        keys_now, values_now = fetch(hop_index)
        key_acc, value_acc = (
            shifted_2(key_acc.astype(jnp.bfloat16), "dp", 1).astype(key_acc.dtype),
            shifted_2(value_acc.astype(jnp.bfloat16), "dp", 1).astype(value_acc.dtype),
        )
        add_query, add_key, add_value = grad_terms(
            queries, keys_now, values_now, hop_index <= group_pos, log_total, d_context, delta_row
        )
        return (
            keys_now,
            values_now,
            key_acc + add_key,
            value_acc + add_value,
            query_acc + add_query,
        )

    back_state = lax.fori_loop(
        1, SEQ_DEV, back_step, (keys_own, values_own, own_key, own_value, own_query)
    )
    key_back, value_back = (
        shifted_2(back_state[2].astype(jnp.bfloat16), "dp", 1 - SEQ_DEV).astype(jnp.float32),
        shifted_2(back_state[3].astype(jnp.bfloat16), "dp", 1 - SEQ_DEV).astype(jnp.float32),
    )
    width_local = local_heads * HEAD_DIM
    d_query = back_state[4].astype(jnp.bfloat16).reshape(row_count, width_local)
    d_key = key_back.astype(jnp.bfloat16).reshape(row_count, width_local)
    d_value = value_back.astype(jnp.bfloat16).reshape(row_count, width_local)
    grad_query = contract_rows(n_one, d_query)
    grad_key = contract_rows(n_one, d_key)
    grad_value = contract_rows(n_one, d_value)
    d_n_part = (
        contract_cols(d_query, w_query)
        + contract_cols(d_key, w_key)
        + contract_cols(d_value, w_value)
    )
    d_n_one = lax.psum(d_n_part.astype(jnp.bfloat16), "tensor").astype(jnp.float32)
    d_input_norm, grad_ln1_gain, grad_ln1_bias = norm_backward(
        d_n_one, normed_one, inverse_one, ln1_gain
    )
    input_grad = d_hidden + d_input_norm
    summed = (
        lax.psum_scatter(grad_ln1_gain, "dp", scatter_dimension=0, tiled=True),
        lax.psum_scatter(grad_ln1_bias, "dp", scatter_dimension=0, tiled=True),
        lax.psum_scatter(grad_query, "dp", scatter_dimension=0, tiled=True),
        lax.psum_scatter(grad_key, "dp", scatter_dimension=0, tiled=True),
        lax.psum_scatter(grad_value, "dp", scatter_dimension=0, tiled=True),
        lax.psum_scatter(grad_out, "dp", scatter_dimension=1, tiled=True),
        lax.psum_scatter(grad_ln2_gain, "dp", scatter_dimension=0, tiled=True),
        lax.psum_scatter(grad_ln2_bias, "dp", scatter_dimension=0, tiled=True),
        lax.psum_scatter(grad_up, "dp", scatter_dimension=0, tiled=True),
        lax.psum_scatter(grad_down, "dp", scatter_dimension=1, tiled=True),
    )
    return (
        output,
        loss_value,
        input_grad,
        summed[0],
        summed[1],
        summed[2],
        summed[3],
        summed[4],
        summed[5],
        summed[6],
        summed[7],
        summed[8],
        summed[9],
    )


def solution(mesh):
    return jax.shard_map(
        per_device,
        mesh=mesh,
        in_specs=(
            P("dp", None),
            P(),
            P(),
            P(None, "tensor"),
            P(None, "tensor"),
            P(None, "tensor"),
            P("tensor", None),
            P(),
            P(),
            P(None, "tensor"),
            P("tensor", None),
            P("dp", None),
            P("dp"),
        ),
        out_specs=(
            P("dp", None),
            P(),
            P("dp", None),
            P("dp"),
            P("dp"),
            P("dp", "tensor"),
            P("dp", "tensor"),
            P("dp", "tensor"),
            P("tensor", "dp"),
            P("dp"),
            P("dp"),
            P("dp", "tensor"),
            P("tensor", "dp"),
        ),
        check_vma=False,
    )
```

profile of v0, /device:TPU:0, one launch (start us, length us, event | category | flops | bytes accessed | tf_op | source)
XLA Modules:
  0.0 1592.3 jit_solution(13820145027896553157)
XLA Ops:
  30.4 7.6 dynamic_update_slice.21
  38.0 6.5 dynamic_update_slice.22
  44.5 337.3 %while.70 = (s32[]{:T(128)}, bf16[512,4,128]{2,1,0:T(4,128)(2,1)}, bf16[512,4,128]{2,1,0:T(4,128)(2,1)}, bf16[16,512,4,128]{3,2,1,0:T(4,128)(2,1)}, bf16[16,512,...) while((s32[]{:T(128)}, bf16[512,4,128]{2,1,0:T(4,128)(2,1)}, bf16[512,4,128]{2,1,0:T(4,128)(2,1)}, ...), condition=%wide.region_5.6_spmd, body=%wide.region_4.5_spmd.sunk | while | flops 5 | bytes 8388823 | solution.py:153
  48.2 4.5 collective-permute-start.1
  60.8 10.0 collective-permute-start
  70.8 4.4 collective-permute-start.1
  83.3 10.0 collective-permute-start
  93.3 4.4 collective-permute-start.1
  105.7 10.0 collective-permute-start
  115.7 4.4 collective-permute-start.1
  128.2 10.0 collective-permute-start
  138.2 4.4 collective-permute-start.1
  150.7 10.0 collective-permute-start
  160.7 4.4 collective-permute-start.1
  173.2 10.0 collective-permute-start
  195.7 10.0 collective-permute-start
  205.7 4.4 collective-permute-start.1
  218.2 10.9 collective-permute-start
  229.0 4.4 collective-permute-start.1
  241.5 10.9 collective-permute-start
  252.4 4.4 collective-permute-start.1
  264.9 10.9 collective-permute-start
  288.3 10.9 collective-permute-start
  299.2 4.4 collective-permute-start.1
  311.7 10.9 collective-permute-start
  322.6 4.4 collective-permute-start.1
  335.0 10.9 collective-permute-start
  358.4 10.9 collective-permute-start
  381.8 8.9 copy.83
  390.7 42.6 %while.71 = (s32[]{:T(128)}, f32[4,512]{1,0:T(4,128)S(1)}, f32[4,512]{1,0:T(4,128)S(1)}, s32[]{:T(128)}, bf16[16,512,4,128]{3,1,2,0:T(8,128)(2,1)}, /*index=5*/b...) while((s32[]{:T(128)}, f32[4,512]{1,0:T(4,128)S(1)}, f32[4,512]{1,0:T(4,128)S(1)}, s32[]{:T(128)}, ...), condition=%wide.region_9.10_spmd, body=%wide.region_6.9_spmd.sunk | while | flops 275779584 | bytes 9543830 | solution.py:168
  433.4 4.6 convolution_bitcast_fusion.1
  438.0 122.7 %while.72 = (s32[]{:T(128)}, f32[512,4,128]{0,2,1:T(8,128)}, bf16[16,512,4,128]{3,2,1,0:T(4,128)(2,1)}, s32[]{:T(128)}, bf16[16,512,4,128]{3,1,2,0:T(8,128)(2,1)...) while((s32[]{:T(128)}, f32[512,4,128]{0,2,1:T(8,128)}, ...), condition=%wide.region_11.12_spmd, body=%wide.region_10.11_spmd.sunk | while | flops 541327360 | bytes 5775521 | solution.py:178
  564.5 55.8 %all-reduce.12.cloned.1.call-done = bf16[512,1024]{1,0:T(8,128)(2,1)} async-done(((bf16[512,1024]{1,0:T(8,128)(2,1)}), bf16[512,1024]{1,0:T(8,128)(2,1)}) %all-reduce.12.cloned.1.call-update) | async-done | bytes 1048592 | tf_op jit(solution)/shard_map/psum | solution.py:180
  631.9 33.9 %psum.45 = f32[]{:T(128)} all-reduce(f32[]{:T(128)} %convert_reduce_fusion.2), channel_id=1, replica_groups=mesh['dp'=16,'tensor'=2] {'dp'}, use_global_device_ids=true, to_apply=%region_19.20 | all-reduce | flops 1 | bytes 8 | tf_op jit(solution)/shard_map/psum | solution.py:191
  666.5 4.9 all-reduce.14.cloned.1.call-done
  671.4 4.9 fusion.58
  684.4 40.2 %all-reduce.16.cloned.1.call-done = bf16[512,1024]{1,0:T(8,128)(2,1)} async-done(((bf16[512,1024]{1,0:T(8,128)(2,1)}), bf16[512,1024]{1,0:T(8,128)(2,1)}) %all-reduce.16.cloned.1.call-update) | async-done | bytes 1048592 | tf_op jit(solution)/shard_map/psum | solution.py:202
  745.1 302.3 %while.73 = (s32[]{:T(128)}, bf16[512,4,128]{2,0,1:T(8,128)(2,1)}, bf16[512,4,128]{2,0,1:T(8,128)(2,1)}, f32[512,4,128]{0,2,1:T(8,128)}, s32[]{:T(128)}, /*index...) while((s32[]{:T(128)}, bf16[512,4,128]{2,0,1:T(8,128)(2,1)}, ...), condition=%wide.region_24.25_spmd, body=%wide.region_23.24_spmd.sunk | while | flops 1355022336 | bytes 69755272 | solution.py:237
  1055.0 5.9 collective-permute-done.4
  1061.7 4.8 collective-permute-done.5
  1082.9 8.0 fusion.72
  1091.0 8.9 fusion.64
  1107.5 61.5 %all-reduce.6 = (f32[]{:T(128)}, f32[1024]{0:T(1024)S(1)}, f32[1024]{0:T(1024)S(1)}, f32[1024]{0:T(1024)S(1)}, f32[1024]{0:T(1024)S(1)}) all-reduce(f32[]{:T(128)} %get-tuple-element.871, f32[1024]{0:T(1024)S(1)} %get-tuple-element.802, f32[1024]{0:T(1024)S(1)} %get-tuple-element.807, ...), channel_id=1, replica_groups=mesh['dp'=16,'tensor'=2] {'dp'}, use_global_device_ids=true, to_apply=%region_17.18 | all-reduce | flops 4097 | bytes 32776 | tf_op jit(solution)/shard_map/psum | solution.py:191
  1176.0 60.5 %reduce-scatter.13.cloned.1.call-done = f32[512,64]{0,1:T(8,128)} async-done(((f32[512,1024]{0,1:T(8,128)}), f32[512,64]{0,1:T(8,128)}) %reduce-scatter.13.cloned.1.call-update) | async-done | bytes 131088 | tf_op jit(solution)/shard_map/reduce_scatter | solution.py:267
  1236.5 64.8 %reduce-scatter.9.cloned.1.call-done = f32[64,512]{1,0:T(8,128)} async-done(((f32[1024,512]{1,0:T(8,128)}), f32[64,512]{1,0:T(8,128)}) %reduce-scatter.9.cloned.1.call-update) | async-done | bytes 131088 | tf_op jit(solution)/shard_map/reduce_scatter | solution.py:265
  1301.4 65.3 %reduce-scatter.11.cloned.1.call-done = f32[64,512]{1,0:T(8,128)} async-done(((f32[1024,512]{1,0:T(8,128)}), f32[64,512]{1,0:T(8,128)}) %reduce-scatter.11.cloned.1.call-update) | async-done | bytes 131088 | tf_op jit(solution)/shard_map/reduce_scatter | solution.py:266
  1366.7 108.4 %reduce-scatter.15.cloned.1.call-done = f32[64,2048]{1,0:T(8,128)} async-done(((f32[1024,2048]{1,0:T(8,128)}), f32[64,2048]{1,0:T(8,128)}) %reduce-scatter.15.cloned.1.call-update) | async-done | bytes 524304 | tf_op jit(solution)/shard_map/reduce_scatter | solution.py:270
  1475.0 108.8 %reduce-scatter.17.cloned.1.call-done = f32[2048,64]{0,1:T(8,128)} async-done(((f32[2048,1024]{0,1:T(8,128)}), f32[2048,64]{0,1:T(8,128)}) %reduce-scatter.17.cloned.1.call-update) | async-done | bytes 524304 | tf_op jit(solution)/shard_map/reduce_scatter | solution.py:271
  (665 shorter events, 712.3 us)
Async XLA Ops:
  7.2 613.2 %all-reduce.12.cloned.1.call-start = ((), (), s32[]{:S(2)}) async-start(), calls=%async_computation.6 | async-start | bytes 2097152 | tf_op jit(solution)/shard_map/psum | solution.py:180
  60.8 14.4 collective-permute-start
  83.3 14.4 collective-permute-start
  105.7 14.4 collective-permute-start
  128.2 14.4 collective-permute-start
  150.7 14.4 collective-permute-start
  173.2 14.4 collective-permute-start
  195.7 14.4 collective-permute-start
  218.2 15.3 collective-permute-start
  241.5 15.3 collective-permute-start
  264.9 15.3 collective-permute-start
  288.3 15.3 collective-permute-start
  311.7 15.3 collective-permute-start
  335.0 15.3 collective-permute-start
  358.4 15.3 collective-permute-start
  564.5 106.9 %all-reduce.14.cloned.1.call-start = ((), (), s32[]{:S(2)}) async-start(), calls=%async_computation.7 | async-start | bytes 2097152 | tf_op jit(solution)/shard_map/psum | solution.py:186
  631.2 93.4 %all-reduce.16.cloned.1.call-start = ((), (), s32[]{:S(2)}) async-start(), calls=%async_computation.8 | async-start | bytes 2097152 | tf_op jit(solution)/shard_map/psum | solution.py:202
  684.3 421.1 %all-reduce.18.cloned.1.call-start = ((), (), s32[]{:S(2)}) async-start(), calls=%async_computation.9 | async-start | bytes 2097152 | tf_op jit(solution)/shard_map/psum | solution.py:256
  745.3 12.9 collective-permute-start.2
  745.4 17.2 %collective-permute-start.3 = (bf16[512,4,128]{2,0,1:T(8,128)(2,1)}, bf16[512,4,128]{2,0,1:T(8,128)(2,1)}, u32[]{:S(2)}, u32[]{:S(2)}) collective-permute-start(bf16[512,4,128]{2,0,1:T(8,128)(2,1)} %get-tuple-element.1163), channel_id=1, source_target_pairs={{0,2},{2,4},{4,6},{6,8},{8,10},{10,12},{12,14},{14,16},{16,18},{18... | collective-permute-start | bytes 1572872 | tf_op jit(solution)/shard_map/while/body/eval_jaxpr/ppermute | solution.py:23
  765.5 11.8 collective-permute-start.2
  765.5 17.2 %collective-permute-start.3 = (bf16[512,4,128]{2,0,1:T(8,128)(2,1)}, bf16[512,4,128]{2,0,1:T(8,128)(2,1)}, u32[]{:S(2)}, u32[]{:S(2)}) collective-permute-start(bf16[512,4,128]{2,0,1:T(8,128)(2,1)} %get-tuple-element.1163), channel_id=1, source_target_pairs={{0,2},{2,4},{4,6},{6,8},{8,10},{10,12},{12,14},{14,16},{16,18},{18... | collective-permute-start | bytes 1572872 | tf_op jit(solution)/shard_map/while/body/eval_jaxpr/ppermute | solution.py:23
  785.6 11.6 collective-permute-start.2
  785.6 17.2 %collective-permute-start.3 = (bf16[512,4,128]{2,0,1:T(8,128)(2,1)}, bf16[512,4,128]{2,0,1:T(8,128)(2,1)}, u32[]{:S(2)}, u32[]{:S(2)}) collective-permute-start(bf16[512,4,128]{2,0,1:T(8,128)(2,1)} %get-tuple-element.1163), channel_id=1, source_target_pairs={{0,2},{2,4},{4,6},{6,8},{8,10},{10,12},{12,14},{14,16},{16,18},{18... | collective-permute-start | bytes 1572872 | tf_op jit(solution)/shard_map/while/body/eval_jaxpr/ppermute | solution.py:23
  805.7 11.6 collective-permute-start.2
  805.7 17.2 %collective-permute-start.3 = (bf16[512,4,128]{2,0,1:T(8,128)(2,1)}, bf16[512,4,128]{2,0,1:T(8,128)(2,1)}, u32[]{:S(2)}, u32[]{:S(2)}) collective-permute-start(bf16[512,4,128]{2,0,1:T(8,128)(2,1)} %get-tuple-element.1163), channel_id=1, source_target_pairs={{0,2},{2,4},{4,6},{6,8},{8,10},{10,12},{12,14},{14,16},{16,18},{18... | collective-permute-start | bytes 1572872 | tf_op jit(solution)/shard_map/while/body/eval_jaxpr/ppermute | solution.py:23
  825.9 17.2 %collective-permute-start.3 = (bf16[512,4,128]{2,0,1:T(8,128)(2,1)}, bf16[512,4,128]{2,0,1:T(8,128)(2,1)}, u32[]{:S(2)}, u32[]{:S(2)}) collective-permute-start(bf16[512,4,128]{2,0,1:T(8,128)(2,1)} %get-tuple-element.1163), channel_id=1, source_target_pairs={{0,2},{2,4},{4,6},{6,8},{8,10},{10,12},{12,14},{14,16},{16,18},{18... | collective-permute-start | bytes 1572872 | tf_op jit(solution)/shard_map/while/body/eval_jaxpr/ppermute | solution.py:23
  846.0 17.2 %collective-permute-start.3 = (bf16[512,4,128]{2,0,1:T(8,128)(2,1)}, bf16[512,4,128]{2,0,1:T(8,128)(2,1)}, u32[]{:S(2)}, u32[]{:S(2)}) collective-permute-start(bf16[512,4,128]{2,0,1:T(8,128)(2,1)} %get-tuple-element.1163), channel_id=1, source_target_pairs={{0,2},{2,4},{4,6},{6,8},{8,10},{10,12},{12,14},{14,16},{16,18},{18... | collective-permute-start | bytes 1572872 | tf_op jit(solution)/shard_map/while/body/eval_jaxpr/ppermute | solution.py:23
  866.1 11.6 collective-permute-start.2
  866.1 17.2 %collective-permute-start.3 = (bf16[512,4,128]{2,0,1:T(8,128)(2,1)}, bf16[512,4,128]{2,0,1:T(8,128)(2,1)}, u32[]{:S(2)}, u32[]{:S(2)}) collective-permute-start(bf16[512,4,128]{2,0,1:T(8,128)(2,1)} %get-tuple-element.1163), channel_id=1, source_target_pairs={{0,2},{2,4},{4,6},{6,8},{8,10},{10,12},{12,14},{14,16},{16,18},{18... | collective-permute-start | bytes 1572872 | tf_op jit(solution)/shard_map/while/body/eval_jaxpr/ppermute | solution.py:23
  886.3 11.6 collective-permute-start.2
  886.3 17.2 %collective-permute-start.3 = (bf16[512,4,128]{2,0,1:T(8,128)(2,1)}, bf16[512,4,128]{2,0,1:T(8,128)(2,1)}, u32[]{:S(2)}, u32[]{:S(2)}) collective-permute-start(bf16[512,4,128]{2,0,1:T(8,128)(2,1)} %get-tuple-element.1163), channel_id=1, source_target_pairs={{0,2},{2,4},{4,6},{6,8},{8,10},{10,12},{12,14},{14,16},{16,18},{18... | collective-permute-start | bytes 1572872 | tf_op jit(solution)/shard_map/while/body/eval_jaxpr/ppermute | solution.py:23
  906.4 17.2 %collective-permute-start.3 = (bf16[512,4,128]{2,0,1:T(8,128)(2,1)}, bf16[512,4,128]{2,0,1:T(8,128)(2,1)}, u32[]{:S(2)}, u32[]{:S(2)}) collective-permute-start(bf16[512,4,128]{2,0,1:T(8,128)(2,1)} %get-tuple-element.1163), channel_id=1, source_target_pairs={{0,2},{2,4},{4,6},{6,8},{8,10},{10,12},{12,14},{14,16},{16,18},{18... | collective-permute-start | bytes 1572872 | tf_op jit(solution)/shard_map/while/body/eval_jaxpr/ppermute | solution.py:23
  926.6 17.2 %collective-permute-start.3 = (bf16[512,4,128]{2,0,1:T(8,128)(2,1)}, bf16[512,4,128]{2,0,1:T(8,128)(2,1)}, u32[]{:S(2)}, u32[]{:S(2)}) collective-permute-start(bf16[512,4,128]{2,0,1:T(8,128)(2,1)} %get-tuple-element.1163), channel_id=1, source_target_pairs={{0,2},{2,4},{4,6},{6,8},{8,10},{10,12},{12,14},{14,16},{16,18},{18... | collective-permute-start | bytes 1572872 | tf_op jit(solution)/shard_map/while/body/eval_jaxpr/ppermute | solution.py:23
  946.7 17.2 %collective-permute-start.3 = (bf16[512,4,128]{2,0,1:T(8,128)(2,1)}, bf16[512,4,128]{2,0,1:T(8,128)(2,1)}, u32[]{:S(2)}, u32[]{:S(2)}) collective-permute-start(bf16[512,4,128]{2,0,1:T(8,128)(2,1)} %get-tuple-element.1163), channel_id=1, source_target_pairs={{0,2},{2,4},{4,6},{6,8},{8,10},{10,12},{12,14},{14,16},{16,18},{18... | collective-permute-start | bytes 1572872 | tf_op jit(solution)/shard_map/while/body/eval_jaxpr/ppermute | solution.py:23
  966.8 17.2 %collective-permute-start.3 = (bf16[512,4,128]{2,0,1:T(8,128)(2,1)}, bf16[512,4,128]{2,0,1:T(8,128)(2,1)}, u32[]{:S(2)}, u32[]{:S(2)}) collective-permute-start(bf16[512,4,128]{2,0,1:T(8,128)(2,1)} %get-tuple-element.1163), channel_id=1, source_target_pairs={{0,2},{2,4},{4,6},{6,8},{8,10},{10,12},{12,14},{14,16},{16,18},{18... | collective-permute-start | bytes 1572872 | tf_op jit(solution)/shard_map/while/body/eval_jaxpr/ppermute | solution.py:23
  987.0 11.6 collective-permute-start.2
  987.0 17.2 %collective-permute-start.3 = (bf16[512,4,128]{2,0,1:T(8,128)(2,1)}, bf16[512,4,128]{2,0,1:T(8,128)(2,1)}, u32[]{:S(2)}, u32[]{:S(2)}) collective-permute-start(bf16[512,4,128]{2,0,1:T(8,128)(2,1)} %get-tuple-element.1163), channel_id=1, source_target_pairs={{0,2},{2,4},{4,6},{6,8},{8,10},{10,12},{12,14},{14,16},{16,18},{18... | collective-permute-start | bytes 1572872 | tf_op jit(solution)/shard_map/while/body/eval_jaxpr/ppermute | solution.py:23
  1007.1 11.6 collective-permute-start.2
  1007.1 17.2 %collective-permute-start.3 = (bf16[512,4,128]{2,0,1:T(8,128)(2,1)}, bf16[512,4,128]{2,0,1:T(8,128)(2,1)}, u32[]{:S(2)}, u32[]{:S(2)}) collective-permute-start(bf16[512,4,128]{2,0,1:T(8,128)(2,1)} %get-tuple-element.1163), channel_id=1, source_target_pairs={{0,2},{2,4},{4,6},{6,8},{8,10},{10,12},{12,14},{14,16},{16,18},{18... | collective-permute-start | bytes 1572872 | tf_op jit(solution)/shard_map/while/body/eval_jaxpr/ppermute | solution.py:23
  1027.2 17.2 %collective-permute-start.3 = (bf16[512,4,128]{2,0,1:T(8,128)(2,1)}, bf16[512,4,128]{2,0,1:T(8,128)(2,1)}, u32[]{:S(2)}, u32[]{:S(2)}) collective-permute-start(bf16[512,4,128]{2,0,1:T(8,128)(2,1)} %get-tuple-element.1163), channel_id=1, source_target_pairs={{0,2},{2,4},{4,6},{6,8},{8,10},{10,12},{12,14},{14,16},{16,18},{18... | collective-permute-start | bytes 1572872 | tf_op jit(solution)/shard_map/while/body/eval_jaxpr/ppermute | solution.py:23
  1052.9 13.6 collective-permute-start.5
  1069.1 106.9 %reduce-scatter.7.cloned.1.call-start = ((), (), s32[]{:S(2)}) async-start(), calls=%async_computation.10 | async-start | bytes 2228224 | tf_op jit(solution)/shard_map/reduce_scatter | solution.py:264
  1072.3 164.2 %reduce-scatter.13.cloned.1.call-start = ((), (), s32[]{:S(2)}) async-start(), calls=%async_computation.13 | async-start | bytes 2228224 | tf_op jit(solution)/shard_map/reduce_scatter | solution.py:267
  1076.2 225.1 %reduce-scatter.9.cloned.1.call-start = ((), (), s32[]{:S(2)}) async-start(), calls=%async_computation.11 | async-start | bytes 2228224 | tf_op jit(solution)/shard_map/reduce_scatter | solution.py:265
  1079.5 287.2 %reduce-scatter.11.cloned.1.call-start = ((), (), s32[]{:S(2)}) async-start(), calls=%async_computation.12 | async-start | bytes 2228224 | tf_op jit(solution)/shard_map/reduce_scatter | solution.py:266
  1082.6 392.4 %reduce-scatter.15.cloned.1.call-start = ((), (), s32[]{:S(2)}) async-start(), calls=%async_computation.14 | async-start | bytes 8912896 | tf_op jit(solution)/shard_map/reduce_scatter | solution.py:270
  1091.0 492.9 %reduce-scatter.17.cloned.1.call-start = ((), (), s32[]{:S(2)}) async-start(), calls=%async_computation.15 | async-start | bytes 8912896 | tf_op jit(solution)/shard_map/reduce_scatter | solution.py:271
  (131 other events, 1624.4 us)
Sparse Core Ops, SparseCore 0:
  564.6 55.7 all-reduce.11
  631.3 40.0 all-reduce.13
  684.4 40.0 all-reduce.15
  1069.2 36.1 all-reduce.17
  1109.5 61.7 reduce-scatter.6
  1175.9 60.5 reduce-scatter.12
  1240.8 60.4 reduce-scatter.8
  1306.1 60.4 reduce-scatter.10
  1371.3 103.6 reduce-scatter.14
  1479.5 104.3 reduce-scatter.16
where the time goes:
time: 1610 us; the launch traced here: 1590 us
  waiting for transfers between devices  563 us (35%)
  matrix products  369 us (23%)
  local copies, waits for them, and re-layouts  288 us (18%)
  starting transfers between devices  218 us (14%)
  blocking collectives  95.4 us (6%)
  other arithmetic  38.4 us (2%)
  between operations  18.9 us (1%)
    ppermute x30, starting transfers between devices, shifted(): lax.ppermute(value, axis, [(source, source + steps) for source in range(l...  216 us
    reduce_scatter x1, waiting for transfers between devices, per_device(): lax.psum_scatter(grad_down, 'dp', scatter_dimension=1, tiled=True)  109 us
    reduce_scatter x1, waiting for transfers between devices, per_device(): lax.psum_scatter(grad_up, 'dp', scatter_dimension=0, tiled=True)  108 us
    psum x2, blocking collectives, per_device(): lax.psum((jnp.sum(weight_rows[:, None] * misfit * misfit), jnp.sum(weight...  95.4 us
    while x165, local copies, waits for them, and re-layouts  90 us
    dynamic_slice x45, local copies, waits for them, and re-layouts, fetch(): lax.dynamic_index_in_dim(value_store, hop_index, 0, keepdims=False)  80.2 us
    dot_general x16, matrix products, value_add(): jnp.einsum('hqk,khe->qhe', prob_rows, values_now, preferred_element_type=...  65.5 us
    reduce_scatter x1, waiting for transfers between devices, per_device(): lax.psum_scatter(grad_value, 'dp', scatter_dimension=0, tiled=True)  65.3 us
  transfers between devices with their start and end apart: 72, of which 39 were waited for; matrix products, arithmetic and copies ran while one was open for 17% of the time, Pallas kernels for 0%

commit v1 on v0

v1 whole, which is shorter than its diff:
```python
import functools

import jax
import jax.numpy as jnp
from jax import lax
from jax.experimental import pallas as pl
from jax.experimental.pallas import tpu as pltpu
from jax.sharding import PartitionSpec as P

HEAD_DIM = 128
SEQ_DEV = 16
EPSILON = 1e-05
NEGATIVE = -1e30
LOG_SCALE = 1.4426950408889634 * HEAD_DIM ** (-0.5)
HEAD_SCALE = HEAD_DIM ** (-0.5)
CHUNKS = 4
f32 = jnp.float32
bf16 = jnp.bfloat16


def nn(a, b):
    return lax.dot_general(a, b, (((1,), (0,)), ((), ())), preferred_element_type=f32)


def nt(a, b):
    return lax.dot_general(a, b, (((1,), (1,)), ((), ())), preferred_element_type=f32)


def tn(a, b):
    return lax.dot_general(a, b, (((0,), (0,)), ((), ())), preferred_element_type=f32)


def remote(src, dst, send_sem, recv_sem, device):
    return pltpu.make_async_remote_copy(
        src_ref=src,
        dst_ref=dst,
        send_sem=send_sem,
        recv_sem=recv_sem,
        device_id=device,
        device_id_type=pl.DeviceIdType.MESH,
    )


class Place:
    def __init__(self):
        index = lax.axis_index("dp")
        self.pos = lax.rem(index, SEQ_DEV)
        self.base = index - self.pos
        self.slab = lax.div(self.pos, 4)
        self.seat = lax.rem(self.pos, 4)
        self.side = lax.axis_index("tensor")
        seat = self.seat
        self.core_seat = seat + 1 - 2 * lax.rem(seat, 2)
        self.x_seat = lax.rem(seat + 2, 4)
        self.far_seat = 3 - seat

    def dev(self, slab, seat):
        return {"dp": self.base + slab * 4 + seat, "tensor": self.side}

    def other_side(self):
        return {"dp": self.base + self.pos, "tensor": 1 - self.side}

    def turned(self, slab):
        even = lax.rem(slab, 2) == 0
        return jnp.where(even, self.seat, self.far_seat)

    def peers(self, same, far, near, side):
        found = []
        for step in range(1, 4):
            other = lax.rem(self.slab + step, 4)
            if same:
                found.append(self.dev(other, self.seat))
            if far:
                found.append(self.dev(other, self.far_seat))
        if far:
            found.append(self.dev(self.slab, self.far_seat))
        if near:
            found.append(self.dev(self.slab, self.core_seat))
            found.append(self.dev(self.slab, self.x_seat))
        if side:
            found.append(self.other_side())
        return found


def greet(peers):
    barrier = pltpu.get_barrier_semaphore()
    for peer in peers:
        pl.semaphore_signal(
            barrier, inc=1, device_id=peer, device_id_type=pl.DeviceIdType.MESH
        )
    return functools.partial(pl.semaphore_wait, barrier, len(peers))


def norm_stats(values):
    average = jnp.mean(values, axis=-1, keepdims=True)
    centred = values - average
    inverse = lax.rsqrt(jnp.mean(centred * centred, axis=-1, keepdims=True) + EPSILON)
    return centred * inverse, inverse


class Summed:
    def __init__(self, at, tile, core_in, x_buf, x_in, z_buf, z_in, send, recv):
        self.at, self.tile = at, tile
        self.core_in, self.x_buf, self.x_in = core_in, x_buf, x_in
        self.z_buf, self.z_in = z_buf, z_in
        self.send, self.recv = send, recv

    def hop(self, src, dst, k, device):
        return remote(src, dst, self.send.at[k], self.recv.at[k], device)

    def near(self):
        at = self.at
        return self.hop(self.tile, self.core_in, 0, at.dev(at.slab, at.core_seat))

    def wide(self):
        at = self.at
        return self.hop(self.x_buf, self.x_in, 1, at.dev(at.slab, at.x_seat))

    def far(self, step):
        at = self.at
        device = at.dev(lax.rem(at.slab + step, 4), at.seat)
        return self.hop(self.z_buf, self.z_in.at[at.slab], 1 + step, device)

    def one(self):
        self.near().start()

    def two(self):
        self.near().wait()
        self.x_buf[...] = self.tile[...] + self.core_in[...]
        self.wide().start()

    def three(self):
        self.wide().wait()
        total = self.x_buf[...] + self.x_in[...]
        self.z_buf[...] = total
        self.z_in[self.at.slab] = total
        for step in range(1, 4):
            self.far(step).start()

    def four(self):
        at = self.at
        for step in range(1, 4):
            self.far(step).wait_send()
            source = lax.rem(at.slab - step + 4, 4)
            slot = self.z_in.at[source]
            self.hop(slot, slot, 1 + step, at.dev(source, at.seat)).wait_recv()
        return (self.z_in[0] + self.z_in[1]) + (self.z_in[2] + self.z_in[3])


def summed_scratch(shape):
    return [
        pltpu.VMEM(shape, f32),
        pltpu.VMEM(shape, f32),
        pltpu.VMEM(shape, f32),
        pltpu.VMEM(shape, f32),
        pltpu.VMEM(shape, f32),
        pltpu.VMEM((4,) + shape, f32),
        pltpu.SemaphoreType.DMA((5,)),
        pltpu.SemaphoreType.DMA((5,)),
    ]


def forward_kernel(
    x_ref, gain_ref, bias_ref, wq_ref, wk_ref, wv_ref, wo_ref, mask_ref,
    none_ref, kv_ref, q_ref, ot_ref, ls_ref, ctx_ref, cnt_ref, wo_in_ref,
    kvs, qs, os, top, low,
    z_send, z_recv, q_send, q_recv, c_send, c_recv, x_send, x_recv, f_send, f_recv,
    o_send, o_recv, w_sem,
    tile, core_in, x_buf, x_in, z_buf, z_in, t_send, t_recv,
):
    at = Place()
    rows = x_ref.shape[0]
    slab, seat = at.slab, at.seat
    ready = greet(at.peers(True, True, True, True))

    def block(kv_slab, kv_seat):
        return kv_ref.at[:, pl.ds(pl.multiple_of((kv_slab * 4 + kv_seat) * rows, rows), rows), :]

    normed, _ = norm_stats(x_ref[...])
    n_one = (normed * gain_ref[...] + bias_ref[...]).astype(bf16)
    none_ref[...] = n_one
    query = nn(n_one, wq_ref[...]).astype(bf16)
    for h in range(4):
        qs[h] = query[:, h * HEAD_DIM : (h + 1) * HEAD_DIM]
    for j, w_ref in enumerate((wk_ref, wv_ref)):
        made = nn(n_one, w_ref[...]).astype(bf16)
        for h in range(4):
            kvs[h, j] = made[:, h * HEAD_DIM : (h + 1) * HEAD_DIM]
    count = jnp.sum(mask_ref[...].astype(f32), axis=1, keepdims=True)
    tile[...] = jnp.broadcast_to(count, tile.shape)
    total = Summed(at, tile, core_in, x_buf, x_in, z_buf, z_in, t_send, t_recv)
    ready()

    def order(k):
        down = jnp.where(3 - k > slab, 3 - k, 2 - k)
        up = jnp.where(k < slab, k, k + 1)
        return jnp.where(slab < 2, down, up)

    goal = at.turned(slab)
    even = lax.rem(slab, 2) == 0

    def q_copy(h):
        return remote(qs.at[h], q_ref.at[slab], q_send.at[h], q_recv.at[slab], at.dev(h, goal))

    def kv_copy(h):
        return remote(
            kvs.at[h], block(slab, seat), z_send.at[h], z_recv.at[slab], at.dev(h, seat)
        )

    def near_copy(kv_slab):
        part = block(kv_slab, seat)
        return remote(
            part, part, c_send.at[kv_slab], c_recv.at[kv_slab], at.dev(slab, at.core_seat)
        )

    def wide_copy(kv_slab):
        part = block(kv_slab, seat)
        return remote(part, part, x_send.at[kv_slab], x_recv.at[kv_slab], at.dev(slab, at.x_seat))

    def pass_copy(kv_slab):
        part = block(kv_slab, at.x_seat)
        return remote(
            part, part, f_send.at[kv_slab], f_recv.at[kv_slab], at.dev(slab, at.core_seat)
        )

    for k in range(3):
        q_copy(order(k)).start()

    @pl.when(even)
    def _():
        q_ref[slab] = qs[slab]

    @pl.when(jnp.logical_not(even))
    def _():
        q_copy(slab).start()

    for k in range(3):
        kv_copy(order(k)).start()
    own = pl.ds(pl.multiple_of(at.pos * rows, rows), rows)
    kv_ref[:, own, :] = kvs[slab]
    near_copy(slab).start()
    wide_copy(slab).start()
    w_copy = remote(wo_ref, wo_in_ref, w_sem.at[0], w_sem.at[1], at.other_side())
    w_copy.start()
    total.one()
    top[...] = jnp.full_like(top, NEGATIVE)
    low[...] = jnp.zeros_like(low)
    ot_ref[...] = jnp.zeros_like(ot_ref)

    def relay(kv_slab):
        @pl.when(slab != kv_slab)
        def _():
            part = block(kv_slab, seat)
            remote(
                part, part, z_send.at[kv_slab], z_recv.at[kv_slab], at.dev(kv_slab, seat)
            ).wait_recv()
            near_copy(kv_slab).start()
            wide_copy(kv_slab).start()

    def arrive(kv_slab):
        part = block(kv_slab, at.x_seat)
        remote(
            part, part, x_send.at[kv_slab], x_recv.at[kv_slab], at.dev(slab, at.x_seat)
        ).wait_recv()
        pass_copy(kv_slab).start()
        part = block(kv_slab, at.core_seat)
        remote(
            part, part, c_send.at[kv_slab], c_recv.at[kv_slab], at.dev(slab, at.core_seat)
        ).wait_recv()
        part = block(kv_slab, at.far_seat)
        remote(
            part, part, f_send.at[kv_slab], f_recv.at[kv_slab], at.dev(slab, at.core_seat)
        ).wait_recv()

    def unit(slot, start, size, diagonal):
        keys_at = pl.ds(pl.multiple_of(start, rows), size)
        scores = nt(kv_ref[0, keys_at, :], q_ref[slot]) * LOG_SCALE
        if diagonal:
            allowed = lax.broadcasted_iota(jnp.int32, scores.shape, 0) <= lax.broadcasted_iota(
                jnp.int32, scores.shape, 1
            )
            scores = jnp.where(allowed, scores, NEGATIVE)
        before = top[slot]
        after = jnp.maximum(before, jnp.max(scores, axis=0, keepdims=True))
        prob = jnp.exp2(scores - after)
        shrink = jnp.exp2(before - after)
        low[slot] = low[slot] * shrink + jnp.sum(prob, axis=0, keepdims=True)
        top[slot] = after
        ot_ref[slot] = ot_ref[slot] * shrink + tn(kv_ref[1, keys_at, :], prob.astype(bf16))

    def o_copy(slot):
        return remote(
            os.at[slot], ctx_ref.at[slab], o_send.at[slot], o_recv.at[slab],
            at.dev(slot, at.turned(slot)),
        )

    for step in range(1, 4):
        source = lax.rem(slab + step, 4)
        part = q_ref.at[source]
        remote(
            part, part, q_send.at[source], q_recv.at[source], at.dev(source, seat)
        ).wait_recv()

    @pl.when(jnp.logical_not(even))
    def _():
        part = q_ref.at[slab]
        remote(part, part, q_send.at[slab], q_recv.at[slab], at.dev(slab, seat)).wait_recv()

    relay(0)
    for kv_slab in range(4):
        arrive(kv_slab)
        first = kv_slab * 4 * rows
        mine = at.turned(kv_slab)

        def whole(index, _):
            unit(kv_slab, first + index * rows, rows, False)
            return 0

        lax.fori_loop(0, mine, whole, 0)
        unit(kv_slab, first + mine * rows, rows, True)
        done = ot_ref[kv_slab] / low[kv_slab]
        ot_ref[kv_slab] = done
        ls_ref[kv_slab] = top[kv_slab] + jnp.log2(low[kv_slab])
        os[kv_slab] = done.T.astype(bf16)
        home = jnp.logical_and(slab == kv_slab, even)

        @pl.when(home)
        def _():
            ctx_ref[slab] = os[kv_slab]

        @pl.when(jnp.logical_not(home))
        def _():
            o_copy(kv_slab).start()

        if kv_slab == 0:
            total.two()
        if kv_slab == 1:
            total.three()
        if kv_slab < 3:
            relay(kv_slab + 1)

            def pair(index, _):
                slot = kv_slab + 1 + lax.div(index, 2)
                unit(slot, first + lax.rem(index, 2) * 2 * rows, 2 * rows, False)
                return 0

            lax.fori_loop(0, 2 * (3 - kv_slab), pair, 0)
    cnt_ref[...] = total.four()
    for k in range(3):
        q_copy(order(k)).wait_send()
        kv_copy(order(k)).wait_send()

    @pl.when(jnp.logical_not(even))
    def _():
        q_copy(slab).wait_send()

    for kv_slab in range(4):
        near_copy(kv_slab).wait_send()
        wide_copy(kv_slab).wait_send()
        pass_copy(kv_slab).wait_send()
        home = jnp.logical_and(slab == kv_slab, even)

        @pl.when(jnp.logical_not(home))
        def _():
            o_copy(kv_slab).wait_send()

        part = ctx_ref.at[kv_slab]
        local = jnp.logical_and(slab == kv_slab, even)

        @pl.when(jnp.logical_not(local))
        def _():
            remote(
                part, part, o_send.at[kv_slab], o_recv.at[kv_slab], at.dev(kv_slab, seat)
            ).wait_recv()

    w_copy.wait()


def heads_row(ref, rows_at):
    return jnp.concatenate([ref[h, rows_at, :] for h in range(4)], axis=1)


def middle_kernel(
    token_total,
    ctx_ref, x_hbm, wo_hbm, wo_in_hbm, gain_ref, bias_ref, wup_hbm, wdn_hbm, teach_hbm,
    mask_ref, cnt_ref,
    out_ref, dh_ref, do_ref, gf_ref, go_ref, vec_ref,
    x_buf, wo, wo_in, wup, wdn, teach, load,
    ctx_in, normed_s, inv_s, n2s, acts, gfs, dpres, gas, dcs,
    fs, fr, bs, br,
    e_send, e_recv, f_send, f_recv, b_send, b_recv, d_send, d_recv,
):
    at = Place()
    slab, seat = at.slab, at.seat
    rows = out_ref.shape[0]
    part_rows = rows // CHUNKS
    ready = greet(at.peers(True, True, False, True))
    loads = [
        pltpu.make_async_copy(src, dst, load.at[k])
        for k, (src, dst) in enumerate(
            (
                (wo_hbm, wo), (wo_in_hbm, wo_in), (x_hbm, x_buf), (wup_hbm, wup),
                (wdn_hbm, wdn), (teach_hbm, teach),
            )
        )
    ]
    for copy in loads:
        copy.start()
    ready()

    def e_copy(c):
        part = pl.ds(pl.multiple_of(c * part_rows, part_rows), part_rows)
        return remote(
            ctx_ref.at[:, part, :], ctx_in.at[:, part, :], e_send.at[c], e_recv.at[c],
            at.other_side(),
        )

    def f_copy(c):
        return remote(fs.at[c], fr.at[c], f_send.at[c], f_recv.at[c], at.other_side())

    def b_copy(c):
        return remote(bs.at[c], br.at[c], b_send.at[c], b_recv.at[c], at.other_side())

    for c in range(CHUNKS):
        e_copy(c).start()
    for k in range(3):
        loads[k].wait()

    def forward(c, _):
        part = pl.ds(pl.multiple_of(c * part_rows, part_rows), part_rows)
        e_copy(c).wait()
        hidden = x_buf[part, :] + (
            nn(heads_row(ctx_ref, part), wo[...]) + nn(heads_row(ctx_in, part), wo_in[...])
        )
        out_ref[part, :] = hidden
        normed, inverse = norm_stats(hidden)
        normed_s[part, :] = normed
        inv_s[part, :] = inverse
        n_two = (normed * gain_ref[...] + bias_ref[...]).astype(bf16)
        n2s[part, :] = n_two

        @pl.when(c == 0)
        def _():
            loads[3].wait()
            loads[4].wait()

        active = jnp.maximum(nn(n_two, wup[...]), 0.0).astype(bf16)
        acts[part, :] = active
        fs[c] = nn(active, wdn[...]).astype(bf16)
        f_copy(c).start()
        return 0

    lax.fori_loop(0, CHUNKS, forward, 0)
    loads[5].wait()
    scale = token_total / cnt_ref[0:1, 0:1]
    vec_ref[...] = jnp.zeros_like(vec_ref)

    def back_one(c, _):
        part = pl.ds(pl.multiple_of(c * part_rows, part_rows), part_rows)
        f_copy(c).wait()
        output = out_ref[part, :] + (fs[c].astype(f32) + fr[c].astype(f32))
        out_ref[part, :] = output
        misfit = output - teach[part, :]
        held = misfit * mask_ref[part, :]
        vec_ref[2:3, :] += jnp.sum(held * misfit, axis=0, keepdims=True)
        d_output = scale * held
        dh_ref[part, :] = d_output
        g_ffn = d_output.astype(bf16)
        gfs[part, :] = g_ffn
        d_active = nt(g_ffn, wdn[...])
        d_pre = jnp.where(acts[part, :] > 0, d_active, 0.0).astype(bf16)
        dpres[part, :] = d_pre
        bs[c] = nt(d_pre, wup[...]).astype(bf16)
        b_copy(c).start()
        return 0

    lax.fori_loop(0, CHUNKS, back_one, 0)
    half = gf_ref.shape[2]

    def down_grad(k, _):
        cols = pl.ds(pl.multiple_of(k * half, half), half)
        gf_ref[2 + k] = tn(gfs[...], acts[:, cols]).astype(bf16)
        return 0

    lax.fori_loop(0, 2, down_grad, 0)

    def d_copy(c, h):
        part = pl.ds(pl.multiple_of(c * part_rows, part_rows), part_rows)
        return remote(
            dcs.at[h, part, :], do_ref.at[slab, part, :], d_send.at[c, h], d_recv.at[c, slab],
            at.dev(h, at.turned(slab)),
        )

    even = lax.rem(slab, 2) == 0

    def back_two(c, _):
        part = pl.ds(pl.multiple_of(c * part_rows, part_rows), part_rows)
        b_copy(c).wait()
        d_two = bs[c].astype(f32) + br[c].astype(f32)
        normed = normed_s[part, :]
        scaled = d_two * gain_ref[...]
        first = jnp.mean(scaled, axis=-1, keepdims=True)
        second = jnp.mean(scaled * normed, axis=-1, keepdims=True)
        d_hidden = dh_ref[part, :] + inv_s[part, :] * (scaled - first - normed * second)
        vec_ref[0:1, :] += jnp.sum(d_two * normed, axis=0, keepdims=True)
        vec_ref[1:2, :] += jnp.sum(d_two, axis=0, keepdims=True)
        dh_ref[part, :] = d_hidden
        g_attn = d_hidden.astype(bf16)
        gas[part, :] = g_attn
        d_context = nt(g_attn, wo[...]).astype(bf16)
        for h in range(4):
            dcs[h, part, :] = d_context[:, h * HEAD_DIM : (h + 1) * HEAD_DIM]
            home = jnp.logical_and(slab == h, even)

            @pl.when(home)
            def _():
                do_ref[slab, part, :] = dcs[h, part, :]

            @pl.when(jnp.logical_not(home))
            def _():
                d_copy(c, h).start()

        return 0

    lax.fori_loop(0, CHUNKS, back_two, 0)

    def up_grad(k, _):
        cols = pl.ds(pl.multiple_of(k * half, half), half)
        gf_ref[k] = tn(n2s[...], dpres[:, cols]).astype(bf16)
        return 0

    lax.fori_loop(0, 2, up_grad, 0)
    go_ref[...] = tn(gas[...], heads_row(ctx_ref, slice(None))).astype(bf16)

    def finish(c, _):
        part = pl.ds(pl.multiple_of(c * part_rows, part_rows), part_rows)
        for h in range(4):
            home = jnp.logical_and(slab == h, even)

            @pl.when(jnp.logical_not(home))
            def _():
                d_copy(c, h).wait_send()
                slot = do_ref.at[h, part, :]
                remote(
                    slot, slot, d_send.at[c, h], d_recv.at[c, h], at.dev(h, seat)
                ).wait_recv()

        return 0

    lax.fori_loop(0, CHUNKS, finish, 0)


def backward_kernel(
    kv_ref, q_ref, ot_ref, ls_ref, do_ref,
    dq_ref, dkv_ref,
    grads, acc, delta, near_out, near_in, wide_out, wide_in, home_out, dqs,
    n_send, n_recv, w_send, w_recv, h_send, h_recv, d_send, d_recv,
):
    at = Place()
    slab, seat = at.slab, at.seat
    rows = q_ref.shape[1]
    even = lax.rem(slab, 2) == 0
    ready = greet(at.peers(True, True, True, False))
    acc[...] = jnp.zeros_like(acc)
    for slot in range(4):
        delta[slot] = jnp.sum(do_ref[slot].astype(f32).T * ot_ref[slot], axis=0, keepdims=True)
    ready()

    def unit(slot, start, local, size, diagonal):
        keys_at = pl.ds(pl.multiple_of(start, rows), size)
        keys = kv_ref[0, keys_at, :]
        query = q_ref[slot]
        d_out = do_ref[slot]
        scores = nt(keys, query) * LOG_SCALE - ls_ref[slot]
        if diagonal:
            allowed = lax.broadcasted_iota(jnp.int32, scores.shape, 0) <= lax.broadcasted_iota(
                jnp.int32, scores.shape, 1
            )
            scores = jnp.where(allowed, scores, NEGATIVE)
        prob = jnp.exp2(scores)
        d_probs = nt(kv_ref[1, keys_at, :], d_out)
        d_scores = (prob * (d_probs - delta[slot])).astype(bf16)
        here = pl.ds(pl.multiple_of(local, rows), size)
        grads[1, here, :] += nn(prob.astype(bf16), d_out)
        grads[0, here, :] += nn(d_scores, query)
        acc[slot] += tn(keys, d_scores)

    def block(ref, which):
        return ref[:, pl.ds(pl.multiple_of(which * rows, rows), rows), :]

    def near_copy(kv_slab):
        k = kv_slab
        return remote(
            near_out, near_in.at[k], n_send.at[k], n_recv.at[k], at.dev(slab, at.core_seat)
        )

    def wide_copy(kv_slab):
        k = kv_slab
        return remote(
            wide_out.at[k], wide_in.at[k], w_send.at[k], w_recv.at[k], at.dev(slab, at.x_seat)
        )

    def home_copy(kv_slab):
        k = kv_slab
        return remote(
            home_out.at[k], dkv_ref.at[slab], h_send.at[k], h_recv.at[slab], at.dev(k, seat)
        )

    pair_scale = HEAD_SCALE

    for step, kv_slab in enumerate((3, 2, 1, 0)):
        grads[...] = jnp.zeros_like(grads)
        first = kv_slab * 4 * rows
        mine = at.turned(kv_slab)

        def whole(index, _):
            unit(kv_slab, first + index * rows, index * rows, rows, False)
            return 0

        lax.fori_loop(0, mine, whole, 0)
        unit(kv_slab, first + mine * rows, mine * rows, rows, True)

        def pair(index, _):
            slot = kv_slab + 1 + lax.div(index, 2)
            local = lax.rem(index, 2) * 2 * rows
            unit(slot, first + local, local, 2 * rows, False)
            return 0

        if kv_slab < 3:
            lax.fori_loop(0, 2 * (3 - kv_slab), pair, 0)
            near_copy(kv_slab + 1).wait_send()
        near_out[0] = block(grads, at.core_seat).astype(bf16)
        near_out[1] = block(grads, at.far_seat).astype(bf16)
        near_copy(kv_slab).start()
        near_copy(kv_slab).wait_recv()
        wide_out[kv_slab] = (block(grads, at.x_seat) + near_in[kv_slab, 1].astype(f32)).astype(
            bf16
        )
        wide_copy(kv_slab).start()
        kept = block(grads, seat) + near_in[kv_slab, 0].astype(f32)
        wide_copy(kv_slab).wait_recv()
        kept = kept + wide_in[kv_slab].astype(f32)
        home_out[kv_slab, 0] = (kept[0] * pair_scale).astype(bf16)
        home_out[kv_slab, 1] = kept[1].astype(bf16)

        @pl.when(slab == kv_slab)
        def _():
            dkv_ref[slab] = home_out[kv_slab]

        @pl.when(slab != kv_slab)
        def _():
            home_copy(kv_slab).start()

    near_copy(0).wait_send()

    def d_copy(slot):
        return remote(
            dqs.at[slot], dq_ref.at[slab], d_send.at[slot], d_recv.at[slab],
            at.dev(slot, at.turned(slot)),
        )

    for slot in range(4):
        dqs[slot] = (acc[slot] * HEAD_SCALE).T.astype(bf16)
        home = jnp.logical_and(slab == slot, even)

        @pl.when(home)
        def _():
            dq_ref[slab] = dqs[slot]

        @pl.when(jnp.logical_not(home))
        def _():
            d_copy(slot).start()

    for k in range(4):
        wide_copy(k).wait_send()
        home = jnp.logical_and(slab == k, even)

        @pl.when(slab != k)
        def _():
            home_copy(k).wait_send()
            part = dkv_ref.at[k]
            remote(part, part, h_send.at[k], h_recv.at[k], at.dev(k, seat)).wait_recv()

        @pl.when(jnp.logical_not(home))
        def _():
            d_copy(k).wait_send()
            part = dq_ref.at[k]
            remote(part, part, d_send.at[k], d_recv.at[k], at.dev(k, seat)).wait_recv()


def tail_kernel(
    dq_ref, dkv_ref, n_one_ref, wq_ref, wk_ref, wv_ref, x_ref, gain_ref, dh_ref, vec_ref,
    gf_ref, go_ref,
    ig_ref, rs_ref, vsum_ref,
    ga, rc, s1, rx, s2, rz, bs, br, dcat,
    b_send, b_recv, c_send, c_recv, x_send, x_recv, z_send, z_recv,
    tile, core_in, x_buf, x_in, z_buf, z_in, t_send, t_recv,
):
    at = Place()
    slab, seat = at.slab, at.seat
    core = lax.rem(seat, 2)
    wide = lax.div(seat, 2)
    rows = x_ref.shape[0]
    part_rows = rows // CHUNKS
    pieces = rc.shape[0]
    early = gf_ref.shape[0]
    ready = greet(at.peers(True, False, True, True))

    def source(k):
        return gf_ref.at[k] if k < early else ga.at[k - early]

    def c_copy(k):
        return remote(
            source(k).at[:, :, 1 - core], rc.at[k], c_send.at[k], c_recv.at[k],
            at.dev(slab, at.core_seat),
        )

    def x_copy(k):
        return remote(
            s1.at[k, :, 1 - wide], rx.at[k], x_send.at[k], x_recv.at[k], at.dev(slab, at.x_seat)
        )

    def z_copy(k, step):
        to = lax.rem(slab + step, 4)
        return remote(
            s2.at[k, to], rz.at[k, step - 1], z_send.at[k, step - 1], z_recv.at[k, step - 1],
            at.dev(to, seat),
        )

    def b_copy(c):
        return remote(bs.at[c], br.at[c], b_send.at[c], b_recv.at[c], at.other_side())

    ready()
    for k in range(early):
        c_copy(k).start()
    dcat[0] = heads_row(dq_ref, slice(None))
    for j in range(2):
        dcat[1 + j] = jnp.concatenate([dkv_ref[h, j] for h in range(4)], axis=1)

    def side_part(c, _):
        part = pl.ds(pl.multiple_of(c * part_rows, part_rows), part_rows)
        bs[c] = (
            nt(dcat[0, part, :], wq_ref[...])
            + nt(dcat[1, part, :], wk_ref[...])
            + nt(dcat[2, part, :], wv_ref[...])
        ).astype(bf16)
        b_copy(c).start()
        return 0

    lax.fori_loop(0, CHUNKS, side_part, 0)
    shape = ga.shape[1:5]
    cols = dcat.shape[2]
    ga[0, :, :, :, :, 0:cols] = go_ref[...]
    for j in range(3):
        made = tn(n_one_ref[...], dcat[j]).astype(bf16).reshape(shape + (cols,))
        k, half = divmod(j + 1, 2)
        ga[k, :, :, :, :, half * cols : (half + 1) * cols] = made
    for k in range(early, pieces):
        c_copy(k).start()

    def add_core(k):
        c_copy(k).wait_recv()

        def one(i, _):
            s1[k, i] = (source(k)[i, :, core].astype(f32) + rc[k, i].astype(f32)).astype(bf16)
            return 0

        lax.fori_loop(0, 4, one, 0)
        x_copy(k).start()

    def add_wide(k):
        x_copy(k).wait_recv()

        def one(i, _):
            s2[k, i] = (s1[k, i, wide].astype(f32) + rx[k, i].astype(f32)).astype(bf16)
            return 0

        lax.fori_loop(0, 4, one, 0)
        for step in range(1, 4):
            z_copy(k, step).start()

    def add_far(k):
        for step in range(1, 4):
            z_copy(k, step).wait_recv()
        rs_ref[k] = (s2[k, slab].astype(f32) + rz[k, 0].astype(f32)) + (
            rz[k, 1].astype(f32) + rz[k, 2].astype(f32)
        )

    for k in range(pieces):
        add_core(k)
    tile[...] = vec_ref[...]
    tile[3:5, :] = jnp.zeros_like(tile[3:5, :])

    def side_sum(c, _):
        part = pl.ds(pl.multiple_of(c * part_rows, part_rows), part_rows)
        b_copy(c).wait()
        d_one = bs[c].astype(f32) + br[c].astype(f32)
        normed, inverse = norm_stats(x_ref[part, :])
        scaled = d_one * gain_ref[...]
        first = jnp.mean(scaled, axis=-1, keepdims=True)
        second = jnp.mean(scaled * normed, axis=-1, keepdims=True)
        ig_ref[part, :] = dh_ref[part, :] + inverse * (scaled - first - normed * second)
        tile[3:4, :] += jnp.sum(d_one * normed, axis=0, keepdims=True)
        tile[4:5, :] += jnp.sum(d_one, axis=0, keepdims=True)
        return 0

    lax.fori_loop(0, CHUNKS, side_sum, 0)
    total = Summed(at, tile, core_in, x_buf, x_in, z_buf, z_in, t_send, t_recv)
    total.one()
    for k in range(pieces):
        add_wide(k)
        if k == 0:
            total.two()
        if k == 1:
            total.three()
    for k in range(pieces):
        add_far(k)
    vsum_ref[...] = total.four()
    for k in range(pieces):
        c_copy(k).wait_send()
        x_copy(k).wait_send()
        for step in range(1, 4):
            z_copy(k, step).wait_send()


def in_vmem():
    return pl.BlockSpec(memory_space=pltpu.VMEM)


def in_hbm():
    return pl.BlockSpec(memory_space=pl.ANY)


def dma(*shape):
    return pltpu.SemaphoreType.DMA(shape)


def call(kernel, name, ident, outs, ins, scratch, args, flops=0):
    return pl.pallas_call(
        kernel,
        name=name,
        out_shape=outs,
        in_specs=ins,
        out_specs=tuple(in_vmem() for _ in outs),
        scratch_shapes=scratch,
        compiler_params=pltpu.CompilerParams(
            collective_id=ident, has_side_effects=True, vmem_limit_bytes=62 * 2**20
        ),
        cost_estimate=pl.CostEstimate(flops=flops, bytes_accessed=2**24, transcendentals=0),
    )(*args)


def per_device(
    inputs, ln1_gain, ln1_bias, w_query, w_key, w_value, w_out, ln2_gain, ln2_bias, w_up, w_down,
    teacher, valid_mask,
):
    rows, width = inputs.shape
    local = w_query.shape[1]
    heads = local // HEAD_DIM
    hidden_units = w_up.shape[1]
    dp_size = lax.axis_size("dp")
    single = dp_size == SEQ_DEV
    share = width // SEQ_DEV
    out = jax.ShapeDtypeStruct
    row = lambda vector: vector.reshape(1, width)
    length = rows * SEQ_DEV
    part_rows = rows // CHUNKS

    n_one, kv_all, q_all, o_t, log_sum, ctx, count, wo_in = call(
        forward_kernel, "forward", 1,
        (
            out((rows, width), bf16),
            out((2, length, HEAD_DIM), bf16),
            out((4, rows, HEAD_DIM), bf16),
            out((4, HEAD_DIM, rows), f32),
            out((4, 1, rows), f32),
            out((heads, rows, HEAD_DIM), bf16),
            out((8, 128), f32),
            out((local, width), bf16),
        ),
        [in_vmem()] * 8,
        [
            pltpu.VMEM((heads, 2, rows, HEAD_DIM), bf16),
            pltpu.VMEM((heads, rows, HEAD_DIM), bf16),
            pltpu.VMEM((4, rows, HEAD_DIM), bf16),
            pltpu.VMEM((4, 1, rows), f32),
            pltpu.VMEM((4, 1, rows), f32),
        ]
        + [dma(4)] * 12
        + [dma(2)]
        + summed_scratch((8, 128)),
        (
            inputs, row(ln1_gain), row(ln1_bias), w_query, w_key, w_value, w_out,
            valid_mask.reshape(1, rows),
        ),
    )
    if not single:
        count = jnp.full((8, 128), lax.psum(jnp.sum(valid_mask.astype(f32)), "dp"))
    output, d_hidden, do_all, grad_ffn, grad_out_t, vectors = call(
        functools.partial(middle_kernel, float(rows * dp_size)), "middle", 2,
        (
            out((rows, width), f32),
            out((rows, width), f32),
            out((4, rows, HEAD_DIM), bf16),
            out((4, width, hidden_units // 2), bf16),
            out((width, local), bf16),
            out((8, width), f32),
        ),
        [
            in_vmem(), in_hbm(), in_hbm(), in_hbm(), in_vmem(), in_vmem(), in_hbm(), in_hbm(),
            in_hbm(), in_vmem(), in_vmem(),
        ],
        [
            pltpu.VMEM((rows, width), f32),
            pltpu.VMEM((local, width), bf16),
            pltpu.VMEM((local, width), bf16),
            pltpu.VMEM((width, hidden_units), bf16),
            pltpu.VMEM((hidden_units, width), bf16),
            pltpu.VMEM((rows, width), f32),
            dma(6),
            pltpu.VMEM((heads, rows, HEAD_DIM), bf16),
            pltpu.VMEM((rows, width), f32),
            pltpu.VMEM((rows, 1), f32),
            pltpu.VMEM((rows, width), bf16),
            pltpu.VMEM((rows, hidden_units), bf16),
            pltpu.VMEM((rows, width), bf16),
            pltpu.VMEM((rows, hidden_units), bf16),
            pltpu.VMEM((rows, width), bf16),
            pltpu.VMEM((heads, rows, HEAD_DIM), bf16),
        ]
        + [pltpu.VMEM((CHUNKS, part_rows, width), bf16)] * 4
        + [dma(CHUNKS)] * 6
        + [dma(CHUNKS, 4)] * 2,
        (
            ctx, inputs, w_out, wo_in, row(ln2_gain), row(ln2_bias), w_up, w_down, teacher,
            valid_mask.astype(f32).reshape(rows, 1), count,
        ),
    )
    d_query, d_kv = call(
        backward_kernel, "backward", 3,
        (
            out((heads, rows, HEAD_DIM), bf16),
            out((heads, 2, rows, HEAD_DIM), bf16),
        ),
        [in_vmem()] * 5,
        [
            pltpu.VMEM((2, 4 * rows, HEAD_DIM), f32),
            pltpu.VMEM((4, HEAD_DIM, rows), f32),
            pltpu.VMEM((4, 1, rows), f32),
            pltpu.VMEM((2, 2, rows, HEAD_DIM), bf16),
            pltpu.VMEM((4, 2, 2, rows, HEAD_DIM), bf16),
            pltpu.VMEM((4, 2, rows, HEAD_DIM), bf16),
            pltpu.VMEM((4, 2, rows, HEAD_DIM), bf16),
            pltpu.VMEM((4, 2, rows, HEAD_DIM), bf16),
            pltpu.VMEM((4, rows, HEAD_DIM), bf16),
        ]
        + [dma(4)] * 8,
        (kv_all, q_all, o_t, log_sum, do_all),
    )
    split = (4, 2, 2, share)
    piece = hidden_units // 2
    extra = (4 * local) // piece
    pieces = 4 + extra
    input_grad, scattered, vector_sums = call(
        tail_kernel, "tail", 4,
        (
            out((rows, width), f32),
            out((pieces, share, piece), f32),
            out((8, width), f32),
        ),
        [in_vmem()] * 12,
        [
            pltpu.VMEM((extra,) + split + (piece,), bf16),
            pltpu.VMEM((pieces, 4, 2, share, piece), bf16),
            pltpu.VMEM((pieces, 4, 2, share, piece), bf16),
            pltpu.VMEM((pieces, 4, share, piece), bf16),
            pltpu.VMEM((pieces, 4, share, piece), bf16),
            pltpu.VMEM((pieces, 3, share, piece), bf16),
            pltpu.VMEM((CHUNKS, part_rows, width), bf16),
            pltpu.VMEM((CHUNKS, part_rows, width), bf16),
            pltpu.VMEM((3, rows, local), bf16),
        ]
        + [dma(CHUNKS)] * 2
        + [dma(pieces)] * 4
        + [dma(pieces, 3)] * 2
        + summed_scratch((8, width)),
        (
            d_query, d_kv, n_one, w_query, w_key, w_value, inputs, row(ln1_gain), d_hidden,
            vectors, grad_ffn.reshape((4,) + split + (piece,)),
            grad_out_t.reshape(split + (local,)),
        ),
    )
    index = lax.axis_index("dp")
    pos = lax.rem(index, SEQ_DEV)
    if not single:
        placed = lax.dynamic_update_slice(
            jnp.zeros((pieces, width, piece), f32), scattered, (0, pos * share, 0)
        )
        scattered = lax.psum_scatter(placed, "dp", scatter_dimension=1, tiled=True)
        vector_sums = lax.psum(jnp.where(pos == 0, vector_sums, 0.0), "dp")
        share = width // dp_size
        pos = index
    grad_up = jnp.concatenate([scattered[0], scattered[1]], axis=1)
    grad_down = jnp.concatenate([scattered[2].T, scattered[3].T], axis=0)
    grad_out = scattered[4][:, :local].T
    grad_query = scattered[4][:, local:]
    grad_key = scattered[5][:, :local]
    grad_value = scattered[5][:, local:]
    loss_value = jnp.sum(vector_sums[2]) / (2.0 * count[0, 0])
    cut = lambda k: lax.dynamic_slice(vector_sums[k], (pos * share,), (share,))
    return (
        output, loss_value, input_grad, cut(3), cut(4), grad_query, grad_key, grad_value, grad_out,
        cut(0), cut(1), grad_up, grad_down,
    )


def solution(mesh):
    return jax.shard_map(
        per_device,
        mesh=mesh,
        in_specs=(
            P("dp", None), P(), P(), P(None, "tensor"), P(None, "tensor"), P(None, "tensor"),
            P("tensor", None), P(), P(), P(None, "tensor"), P("tensor", None), P("dp", None),
            P("dp"),
        ),
        out_specs=(
            P("dp", None), P(), P("dp", None), P("dp"), P("dp"), P("dp", "tensor"),
            P("dp", "tensor"), P("dp", "tensor"), P("tensor", "dp"), P("dp"), P("dp"),
            P("dp", "tensor"), P("tensor", "dp"),
        ),
        check_vma=False,
    )
```

time: 1610 us -> 405 us (0.25); the launches traced: 1590 us -> 405 us
  waiting for transfers between devices: 563 us -> 0 us
  Pallas kernels: 0 us -> 390 us
  matrix products: 369 us -> 0 us
  local copies, waits for them, and re-layouts: 288 us -> 9.13 us
  starting transfers between devices: 218 us -> 0 us
  blocking collectives: 95.4 us -> 0 us
  other arithmetic: 38.4 us -> 2.28 us
    reduce_scatter x6 -> x0, waiting for transfers between devices: 408 us -> none  [the longest x1 109 us: per_device(): lax.psum_scatter(grad_down, 'dp', scatter_dimension=1, tiled=True)]
    pallas_call x0 -> x4, Pallas kernels: none -> 390 us  [call(): pl.pallas_call(kernel, name=name, out_shape=outs, in_specs=ins, out_specs...]
    dot_general x129 -> x0, matrix products: 369 us -> none  [the longest x16 65.5 us: value_add(): jnp.einsum('hqk,khe->qhe', prob_rows, values_now, preferred_element_type=...]
    ppermute x62 -> x0, starting transfers between devices: 218 us -> none  [the longest x30 216 us: shifted(): lax.ppermute(value, axis, [(source, source + steps) for source in range(l...]
    while x174 -> x0, local copies, waits for them, and re-layouts: 114 us -> none
    psum x4 -> x0, waiting for transfers between devices: 104 us -> none  [the longest x1 55.8 us: per_device(): lax.psum(jnp.dot(context, w_out, preferred_element_type=jnp.float32).asty...]
    psum x2 -> x0, blocking collectives: 95.4 us -> none  [per_device(): lax.psum((jnp.sum(weight_rows[:, None] * misfit * misfit), jnp.sum(weight...]
    dynamic_slice x45 -> x2, local copies, waits for them, and re-layouts: 80.2 us -> 1.17 us  [per_device(): cut = lambda k: lax.dynamic_slice(vector_sums[k], (pos * share,), (share,))]
  transfers between devices with their start and end apart: 72 -> 0, of which waited for: 39 -> 0; matrix products, arithmetic and copies ran while one was open for 17% -> 0% of each run, Pallas kernels for 0% -> 0%
where the time goes in v1:
time: 405 us
  Pallas kernels  390 us (96%)
  local copies, waits for them, and re-layouts  9.13 us (2%)
    pallas_call x4, Pallas kernels, call(): pl.pallas_call(kernel, name=name, out_shape=outs, in_specs=ins, out_specs...  390 us

profile of v1, /device:TPU:0, one launch (start us, length us, event | category | flops | bytes accessed | tf_op | source)
XLA Modules:
  0.0 405.1 jit_solution(7090075533998586584)
XLA Ops:
  0.6 0.0 copy-start.3
  0.7 68.9 %forward.1 = (bf16[512,1024]{1,0:T(8,128)(2,1)}, bf16[2,8192,128]{2,1,0:T(8,128)(2,1)}, bf16[4,512,128]{2,1,0:T(8,128)(2,1)}, f32[4,128,512]{2,1,0:T(8,128)}, f3...) custom-call(f32[512,1024]{1,0:T(8,128)} %x_ref.3, ...), custom_call_target="tpu_custom_call" | custom-call | bytes 16777216 | tf_op jit(solution)/shard_map/forward/pallas_call | solution.py:839
  69.6 0.0 copy-done.3
  69.6 0.9 copy.26.mask_ref
  70.5 93.1 %middle.1 = (f32[512,1024]{1,0:T(8,128)}, f32[512,1024]{1,0:T(8,128)}, bf16[4,512,128]{2,1,0:T(8,128)(2,1)}, bf16[4,1024,1024]{2,1,0:T(8,128)(2,1)}, bf16[1024,512]{1,0:T(8,128)(2,1)}, /*index=5*/f32[8,1024]{1,0:T(8,128)}) custom-call(bf16[4,512,128]{2,1,0:T(8,128)(2,1)} %get-tuple-element.32.ctx_ref, f32[512,1024]{1,0:T(8,128)} %x_ref.3, ...), custom_call_target="tpu_custom_call" | custom-call | bytes 16777216 | tf_op jit(solution)/shard_map/middle/pallas_call | solution.py:839
  163.6 97.5 %backward.1 = (bf16[4,512,128]{2,1,0:T(8,128)(2,1)}, bf16[4,2,512,128]{3,2,1,0:T(8,128)(2,1)}) custom-call(bf16[2,8192,128]{2,1,0:T(8,128)(2,1)} %get-tuple-element.36.kv_ref, bf16[4,512,128]{2,1,0:T(8,128)(2,1)} %get-tuple-element.37.q_ref, f32[4,128,512]{2,1,0:T(8,128)} %get-tuple-element.38.ot_ref, f32[4,1,512]{2,1,0:T(1,128)} %get-tuple-element.39.ls_ref, ...), custom_call_target="tpu_custom_call" | custom-call | bytes 16777216 | tf_op jit(solution)/shard_map/backward/pallas_call | solution.py:839
  261.0 131.0 %tail.1 = (f32[512,1024]{1,0:T(8,128)}, f32[6,64,1024]{2,1,0:T(8,128)}, f32[8,1024]{1,0:T(8,128)}) custom-call(bf16[4,512,128]{2,1,0:T(8,128)(2,1)} %get-tuple-element.41.dq_ref, bf16[4,2,512,128]{3,2,1,0:T(8,128)(2,1)} %get-tuple-element.42.dkv_ref, bf16[512,1024]{1,0:T(8,128)(2,1)} %get-tuple-element.43.n_one_ref, bf16[1024,512]{1,0:T(8,128)(2,1)} %wq_ref.3, ...), custom_call_target="tpu_custom_call" | custom-call | bytes 16777216 | tf_op jit(solution)/shard_map/tail/pallas_call | solution.py:839
  392.0 0.0 copy-start.2
  392.0 1.5 slice_bitcast_fusion.1
  393.5 0.0 copy-start
  393.5 0.8 pad_maximum_fusion.1
  394.3 0.8 pad_maximum_fusion
  395.2 0.0 copy-done.2
  395.2 0.6 fusion.5
  395.8 0.6 fusion.2
  396.4 0.8 slice_bitcast_fusion.6
  397.2 0.6 fusion
  397.8 1.2 slice.51
  400.2 0.0 copy-done
  400.2 0.0 copy-start.1
  400.3 1.3 copy.29
  401.6 1.0 copy-done.1
  402.6 1.3 copy.30
  (1 shorter events, 0.0 us)
Async XLA Ops:
  0.6 69.0 %copy-start.3 = (s32[512]{0:T(512)S(1)}, s32[512]{0:T(512)}, u32[]{:S(2)}) copy-start(s32[512]{0:T(512)} %param.25) | copy-start | bytes 6148
  392.0 3.1 copy-start.2
  393.5 6.7 %copy-start = (f32[512,1024]{1,0:T(8,128)S(1)}, f32[512,1024]{1,0:T(8,128)}, u32[]{:S(2)}) copy-start(f32[512,1024]{1,0:T(8,128)} %get-tuple-element.85) | copy-start | bytes 6291460
  400.2 2.3 copy-start.1

commit v2 on v1

v2 whole, which is shorter than its diff:
```python
import functools

import jax
import jax.numpy as jnp
from jax import lax
from jax.experimental import pallas as pl
from jax.experimental.pallas import tpu as pltpu
from jax.sharding import PartitionSpec as P

HEAD_DIM = 128
SEQ_DEV = 16
EPSILON = 1e-05
NEGATIVE = -1e30
LOG_SCALE = 1.4426950408889634 * HEAD_DIM ** (-0.5)
HEAD_SCALE = HEAD_DIM ** (-0.5)
CHUNKS = 4
STEPS = 4
f32 = jnp.float32
bf16 = jnp.bfloat16


def nn(a, b):
    return lax.dot_general(a, b, (((1,), (0,)), ((), ())), preferred_element_type=f32)


def nt(a, b):
    return lax.dot_general(a, b, (((1,), (1,)), ((), ())), preferred_element_type=f32)


def tn(a, b):
    return lax.dot_general(a, b, (((0,), (0,)), ((), ())), preferred_element_type=f32)


def remote(src, dst, send_sem, recv_sem, device):
    return pltpu.make_async_remote_copy(
        src_ref=src,
        dst_ref=dst,
        send_sem=send_sem,
        recv_sem=recv_sem,
        device_id=device,
        device_id_type=pl.DeviceIdType.MESH,
    )


class Place:
    def __init__(self):
        index = lax.axis_index("dp")
        self.pos = lax.rem(index, SEQ_DEV)
        self.base = index - self.pos
        self.slab = lax.div(self.pos, 4)
        self.seat = lax.rem(self.pos, 4)
        self.side = lax.axis_index("tensor")
        seat = self.seat
        self.core_seat = seat + 1 - 2 * lax.rem(seat, 2)
        self.x_seat = lax.rem(seat + 2, 4)
        self.far_seat = 3 - seat

    def dev(self, slab, seat):
        return {"dp": self.base + slab * 4 + seat, "tensor": self.side}

    def other_side(self):
        return {"dp": self.base + self.pos, "tensor": 1 - self.side}

    def turned(self, slab):
        even = lax.rem(slab, 2) == 0
        return jnp.where(even, self.seat, self.far_seat)

    def peers(self, same, far, near, side):
        found = []
        for step in range(1, 4):
            other = lax.rem(self.slab + step, 4)
            if same:
                found.append(self.dev(other, self.seat))
            if far:
                found.append(self.dev(other, self.far_seat))
        if far:
            found.append(self.dev(self.slab, self.far_seat))
        if near:
            found.append(self.dev(self.slab, self.core_seat))
            found.append(self.dev(self.slab, self.x_seat))
        if side:
            found.append(self.other_side())
        return found


def greet(peers):
    barrier = pltpu.get_barrier_semaphore()
    for peer in peers:
        pl.semaphore_signal(
            barrier, inc=1, device_id=peer, device_id_type=pl.DeviceIdType.MESH
        )
    return functools.partial(pl.semaphore_wait, barrier, len(peers))


def norm_stats(values):
    average = jnp.mean(values, axis=-1, keepdims=True)
    centred = values - average
    inverse = lax.rsqrt(jnp.mean(centred * centred, axis=-1, keepdims=True) + EPSILON)
    return centred * inverse, inverse


class Summed:
    def __init__(self, at, tile, core_in, x_buf, x_in, z_buf, z_in, send, recv):
        self.at, self.tile = at, tile
        self.core_in, self.x_buf, self.x_in = core_in, x_buf, x_in
        self.z_buf, self.z_in = z_buf, z_in
        self.send, self.recv = send, recv

    def hop(self, src, dst, k, device):
        return remote(src, dst, self.send.at[k], self.recv.at[k], device)

    def near(self):
        at = self.at
        return self.hop(self.tile, self.core_in, 0, at.dev(at.slab, at.core_seat))

    def wide(self):
        at = self.at
        return self.hop(self.x_buf, self.x_in, 1, at.dev(at.slab, at.x_seat))

    def far(self, step):
        at = self.at
        device = at.dev(lax.rem(at.slab + step, 4), at.seat)
        return self.hop(self.z_buf, self.z_in.at[at.slab], 1 + step, device)

    def one(self):
        self.near().start()

    def two(self):
        self.near().wait()
        self.x_buf[...] = self.tile[...] + self.core_in[...]
        self.wide().start()

    def three(self):
        self.wide().wait()
        total = self.x_buf[...] + self.x_in[...]
        self.z_buf[...] = total
        self.z_in[self.at.slab] = total
        for step in range(1, 4):
            self.far(step).start()

    def four(self):
        at = self.at
        for step in range(1, 4):
            self.far(step).wait_send()
            source = lax.rem(at.slab - step + 4, 4)
            slot = self.z_in.at[source]
            self.hop(slot, slot, 1 + step, at.dev(source, at.seat)).wait_recv()
        return (self.z_in[0] + self.z_in[1]) + (self.z_in[2] + self.z_in[3])


def summed_scratch(shape):
    return [
        pltpu.VMEM(shape, f32),
        pltpu.VMEM(shape, f32),
        pltpu.VMEM(shape, f32),
        pltpu.VMEM(shape, f32),
        pltpu.VMEM(shape, f32),
        pltpu.VMEM((4,) + shape, f32),
        pltpu.SemaphoreType.DMA((5,)),
        pltpu.SemaphoreType.DMA((5,)),
    ]


class Scatter:
    def __init__(self, at, rc, s1, rx, s2, ra, s3, rb, send, recv):
        self.at = at
        self.core = lax.rem(at.seat, 2)
        self.wide = lax.div(at.seat, 2)
        self.low = lax.rem(at.slab, 2)
        self.high = lax.div(at.slab, 2)
        self.rc, self.s1, self.rx, self.s2 = rc, s1, rx, s2
        self.ra, self.s3, self.rb = ra, s3, rb
        self.send, self.recv = send, recv

    def hop(self, stage, k, src, dst, device):
        return remote(src, dst, self.send.at[stage, k], self.recv.at[stage, k], device)

    def c_copy(self, k, source):
        at = self.at
        device = at.dev(at.slab, at.core_seat)
        return self.hop(0, k, source.at[:, :, 1 - self.core], self.rc.at[k], device)

    def x_copy(self, k):
        at = self.at
        device = at.dev(at.slab, at.x_seat)
        return self.hop(1, k, self.s1.at[k, :, 1 - self.wide], self.rx.at[k], device)

    def a_copy(self, k):
        at = self.at
        device = at.dev(at.slab + 1 - 2 * self.low, at.seat)
        return self.hop(2, k, self.s2.at[k, :, 1 - self.low], self.ra.at[k], device)

    def b_copy(self, k):
        at = self.at
        device = at.dev(lax.rem(at.slab + 2, 4), at.seat)
        return self.hop(3, k, self.s3.at[k, 1 - self.high], self.rb.at[k], device)

    def core_add(self, k, source):
        self.c_copy(k, source).wait_recv()

        def one(i, _):
            self.s1[k, i] = (
                source[i, :, self.core].astype(f32) + self.rc[k, i].astype(f32)
            ).astype(bf16)
            return 0

        lax.fori_loop(0, 4, one, 0)

    def x_add(self, k):
        self.x_copy(k).wait_recv()
        for i in range(4):
            self.s2[k, i // 2, i % 2] = (
                self.s1[k, i, self.wide].astype(f32) + self.rx[k, i].astype(f32)
            ).astype(bf16)

    def a_add(self, k):
        self.a_copy(k).wait_recv()
        for i in range(2):
            self.s3[k, i] = (
                self.s2[k, i, self.low].astype(f32) + self.ra[k, i].astype(f32)
            ).astype(bf16)

    def b_add(self, k):
        self.b_copy(k).wait_recv()
        return self.s3[k, self.high].astype(f32) + self.rb[k].astype(f32)


def attend_mask(size, rows, per, step, mine):
    key = lax.broadcasted_iota(jnp.int32, (size, 1), 0)
    key = lax.div(key, per) * rows + lax.rem(key, per) + step * per
    query = lax.broadcasted_iota(jnp.int32, (1, rows), 1) + mine * rows
    return key <= query


def forward_kernel(
    x_ref, gain_ref, bias_ref, wq_ref, wk_ref, wv_ref, wo_ref, mask_ref,
    none_ref, kv_ref, q_ref, ot_ref, ls_ref, ctx_ref, cnt_ref, wo_in_ref,
    kvs, qs, os, top, low,
    z_send, z_recv, q_send, q_recv, c_send, c_recv, x_send, x_recv, f_send, f_recv,
    o_send, o_recv, w_sem,
    tile, core_in, x_buf, x_in, z_buf, z_in, t_send, t_recv,
):
    at = Place()
    rows = x_ref.shape[0]
    per = rows // STEPS
    slab, seat = at.slab, at.seat
    even = lax.rem(slab, 2) == 0
    odd = jnp.logical_not(even)
    goal = at.turned(slab)
    ready = greet(at.peers(True, True, True, True))

    def order(k):
        down = jnp.where(3 - k > slab, 3 - k, 2 - k)
        up = jnp.where(k < slab, k, k + 1)
        return jnp.where(slab < 2, down, up)

    def q_copy(h):
        return remote(qs.at[h], q_ref.at[slab], q_send.at[h], q_recv.at[slab], at.dev(h, goal))

    def kv_copy(h, t):
        return remote(
            kvs.at[h, :, t], kv_ref.at[:, slab, seat, t], z_send.at[t, h], z_recv.at[t, slab],
            at.dev(h, seat),
        )

    def near_copy(t):
        part = kv_ref.at[:, :, seat, t]
        return remote(part, part, c_send.at[t], c_recv.at[t], at.dev(slab, at.core_seat))

    def wide_copy(t):
        part = kv_ref.at[:, :, seat, t]
        return remote(part, part, x_send.at[t], x_recv.at[t], at.dev(slab, at.x_seat))

    def pass_copy(t):
        part = kv_ref.at[:, :, at.x_seat, t]
        return remote(part, part, f_send.at[t], f_recv.at[t], at.dev(slab, at.core_seat))

    normed, _ = norm_stats(x_ref[...])
    n_one = (normed * gain_ref[...] + bias_ref[...]).astype(bf16)
    none_ref[...] = n_one
    query = nn(n_one, wq_ref[...]).astype(bf16)
    for h in range(4):
        qs[h] = query[:, h * HEAD_DIM : (h + 1) * HEAD_DIM]
    ready()
    for k in range(3):
        q_copy(order(k)).start()

    @pl.when(even)
    def _():
        q_ref[slab] = qs[slab]

    @pl.when(odd)
    def _():
        q_copy(slab).start()

    for j, w_ref in enumerate((wk_ref, wv_ref)):
        made = nn(none_ref[...], w_ref[...]).astype(bf16)
        for h in range(4):
            kvs[h, j] = made[:, h * HEAD_DIM : (h + 1) * HEAD_DIM].reshape(STEPS, per, HEAD_DIM)
    for t in range(STEPS):
        for k in range(3):
            kv_copy(order(k), t).start()
    kv_ref[:, slab, seat] = kvs[slab]
    w_copy = remote(wo_ref, wo_in_ref, w_sem.at[0], w_sem.at[1], at.other_side())
    w_copy.start()
    count = jnp.sum(mask_ref[...].astype(f32), axis=1, keepdims=True)
    tile[...] = jnp.broadcast_to(count, tile.shape)
    total = Summed(at, tile, core_in, x_buf, x_in, z_buf, z_in, t_send, t_recv)
    total.one()
    top[...] = jnp.full_like(top, NEGATIVE)
    low[...] = jnp.zeros_like(low)
    ot_ref[...] = jnp.zeros_like(ot_ref)

    def relay(t):
        for step in range(1, 4):
            source = lax.rem(slab + step, 4)
            part = kv_ref.at[:, source, seat, t]
            remote(
                part, part, z_send.at[t, source], z_recv.at[t, source], at.dev(source, seat)
            ).wait_recv()
        near_copy(t).start()
        wide_copy(t).start()

    def hand_on(t):
        part = kv_ref.at[:, :, at.x_seat, t]
        remote(part, part, x_send.at[t], x_recv.at[t], at.dev(slab, at.x_seat)).wait_recv()
        pass_copy(t).start()

    def arrive(t):
        device = at.dev(slab, at.core_seat)
        part = kv_ref.at[:, :, at.core_seat, t]
        remote(part, part, c_send.at[t], c_recv.at[t], device).wait_recv()
        part = kv_ref.at[:, :, at.far_seat, t]
        remote(part, part, f_send.at[t], f_recv.at[t], device).wait_recv()

    def unit(slot, keys, values, allowed):
        scores = nt(keys, q_ref[slot]) * LOG_SCALE
        if allowed is not None:
            scores = jnp.where(allowed, scores, NEGATIVE)
        before = top[slot]
        after = jnp.maximum(before, jnp.max(scores, axis=0, keepdims=True))
        prob = jnp.exp2(scores - after)
        shrink = jnp.exp2(before - after)
        low[slot] = low[slot] * shrink + jnp.sum(prob, axis=0, keepdims=True)
        top[slot] = after
        ot_ref[slot] = ot_ref[slot] * shrink + tn(values, prob.astype(bf16))

    def o_copy(slot):
        return remote(
            os.at[slot], ctx_ref.at[slab], o_send.at[slot], o_recv.at[slab],
            at.dev(slot, at.turned(slot)),
        )

    def slot_step(slot, t):
        if slot > 0:
            size = 4 * slot * per
            unit(
                slot,
                kv_ref[0, 0:slot, :, t].reshape(size, HEAD_DIM),
                kv_ref[1, 0:slot, :, t].reshape(size, HEAD_DIM),
                None,
            )
        mine = at.turned(slot)
        for blocks, chosen in ((2, mine < 2), (4, mine >= 2)):

            @pl.when(chosen)
            def _():
                size = blocks * per
                unit(
                    slot,
                    kv_ref[0, slot, 0:blocks, t].reshape(size, HEAD_DIM),
                    kv_ref[1, slot, 0:blocks, t].reshape(size, HEAD_DIM),
                    attend_mask(size, rows, per, t, mine),
                )

        @pl.when(t == STEPS - 1)
        def _():
            done = ot_ref[slot] / low[slot]
            ot_ref[slot] = done
            ls_ref[slot] = top[slot] + jnp.log2(low[slot])
            os[slot] = done.T.astype(bf16)
            home = jnp.logical_and(slab == slot, even)

            @pl.when(home)
            def _():
                ctx_ref[slab] = os[slot]

            @pl.when(jnp.logical_not(home))
            def _():
                o_copy(slot).start()

    for step in range(1, 4):
        source = lax.rem(slab + step, 4)
        part = q_ref.at[source]
        remote(
            part, part, q_send.at[source], q_recv.at[source], at.dev(source, seat)
        ).wait_recv()

    @pl.when(odd)
    def _():
        part = q_ref.at[slab]
        remote(part, part, q_send.at[slab], q_recv.at[slab], at.dev(slab, seat)).wait_recv()

    relay(0)
    total.two()
    relay(1)
    hand_on(0)

    def go(t, _):
        arrive(t)
        slot_step(3, t)

        @pl.when(t + 2 < STEPS)
        def _():
            relay(t + 2)

        @pl.when(t + 1 < STEPS)
        def _():
            hand_on(t + 1)

        @pl.when(t == 0)
        def _():
            total.three()

        slot_step(0, t)
        slot_step(2, t)
        slot_step(1, t)
        return 0

    lax.fori_loop(0, STEPS, go, 0)
    cnt_ref[...] = total.four()
    for k in range(3):
        q_copy(order(k)).wait_send()

    @pl.when(odd)
    def _():
        q_copy(slab).wait_send()

    def finish(t, _):
        for k in range(3):
            kv_copy(order(k), t).wait_send()
        near_copy(t).wait_send()
        wide_copy(t).wait_send()
        pass_copy(t).wait_send()
        return 0

    lax.fori_loop(0, STEPS, finish, 0)
    w_copy.wait()
    for k in range(4):
        home = jnp.logical_and(slab == k, even)

        @pl.when(jnp.logical_not(home))
        def _():
            o_copy(k).wait_send()
            part = ctx_ref.at[k]
            remote(part, part, o_send.at[k], o_recv.at[k], at.dev(k, seat)).wait_recv()


def heads_row(ref, rows_at):
    return jnp.concatenate([ref[h, rows_at, :] for h in range(4)], axis=1)


def middle_kernel(
    token_total,
    ctx_ref, x_hbm, wo_hbm, wo_in_hbm, gain_ref, bias_ref, wup_hbm, wdn_hbm, teach_hbm,
    mask_ref, cnt_ref,
    out_ref, dh_ref, do_ref, up_ref, dn_ref, go_ref, vec_ref,
    x_buf, wo, wo_in, wup, wdn, teach, load,
    ctx_in, normed_s, inv_s, n2s, acts, gfs, dpres, gas, dcs,
    fs, fr, bs, br,
    e_send, e_recv, f_send, f_recv, b_send, b_recv, d_send, d_recv,
    gt, rc, s1, rx, g_send, g_recv,
):
    at = Place()
    slab, seat = at.slab, at.seat
    rows = out_ref.shape[0]
    part_rows = rows // CHUNKS
    ready = greet(at.peers(True, True, True, True))
    loads = [
        pltpu.make_async_copy(src, dst, load.at[k])
        for k, (src, dst) in enumerate(
            (
                (wo_hbm, wo), (wo_in_hbm, wo_in), (x_hbm, x_buf), (wup_hbm, wup),
                (wdn_hbm, wdn), (teach_hbm, teach),
            )
        )
    ]
    for copy in loads:
        copy.start()
    ready()

    def e_copy(c):
        part = pl.ds(pl.multiple_of(c * part_rows, part_rows), part_rows)
        return remote(
            ctx_ref.at[:, part, :], ctx_in.at[:, part, :], e_send.at[c], e_recv.at[c],
            at.other_side(),
        )

    def f_copy(c):
        return remote(fs.at[c], fr.at[c], f_send.at[c], f_recv.at[c], at.other_side())

    def b_copy(c):
        return remote(bs.at[c], br.at[c], b_send.at[c], b_recv.at[c], at.other_side())

    for c in range(CHUNKS):
        e_copy(c).start()
    for k in range(3):
        loads[k].wait()

    def forward(c, _):
        part = pl.ds(pl.multiple_of(c * part_rows, part_rows), part_rows)
        e_copy(c).wait()
        hidden = x_buf[part, :] + (
            nn(heads_row(ctx_ref, part), wo[...]) + nn(heads_row(ctx_in, part), wo_in[...])
        )
        out_ref[part, :] = hidden
        normed, inverse = norm_stats(hidden)
        normed_s[part, :] = normed
        inv_s[part, :] = inverse
        n_two = (normed * gain_ref[...] + bias_ref[...]).astype(bf16)
        n2s[part, :] = n_two

        @pl.when(c == 0)
        def _():
            loads[3].wait()
            loads[4].wait()

        active = jnp.maximum(nn(n_two, wup[...]), 0.0).astype(bf16)
        acts[part, :] = active
        fs[c] = nn(active, wdn[...]).astype(bf16)
        f_copy(c).start()
        return 0

    lax.fori_loop(0, CHUNKS, forward, 0)
    loads[5].wait()
    scale = token_total / cnt_ref[0:1, 0:1]
    vec_ref[...] = jnp.zeros_like(vec_ref)

    def back_one(c, _):
        part = pl.ds(pl.multiple_of(c * part_rows, part_rows), part_rows)
        f_copy(c).wait()
        output = out_ref[part, :] + (fs[c].astype(f32) + fr[c].astype(f32))
        out_ref[part, :] = output
        misfit = output - teach[part, :]
        held = misfit * mask_ref[part, :]
        vec_ref[2:3, :] += jnp.sum(held * misfit, axis=0, keepdims=True)
        d_output = scale * held
        dh_ref[part, :] = d_output
        g_ffn = d_output.astype(bf16)
        gfs[part, :] = g_ffn
        d_active = nt(g_ffn, wdn[...])
        d_pre = jnp.where(acts[part, :] > 0, d_active, 0.0).astype(bf16)
        dpres[part, :] = d_pre
        bs[c] = nt(d_pre, wup[...]).astype(bf16)
        b_copy(c).start()
        return 0

    lax.fori_loop(0, CHUNKS, back_one, 0)
    scatter = Scatter(at, rc, s1, rx, dn_ref, None, None, None, g_send, g_recv)
    split = gt.shape[1:5]
    half = gt.shape[5] // 2
    for k in range(4):
        slot = gt.at[k % 2]
        if k >= 2:
            scatter.c_copy(k - 2, slot).wait_send()
        for j in range(2):
            cols = slice((k % 2) * 2 * half + j * half, (k % 2) * 2 * half + (j + 1) * half)
            if k < 2:
                made = tn(gfs[...], acts[:, cols])
            else:
                made = tn(n2s[...], dpres[:, cols])
            gt[k % 2, :, :, :, :, j * half : (j + 1) * half] = made.astype(bf16).reshape(
                split + (half,)
            )
        scatter.c_copy(k, slot).start()
        if k >= 1:
            scatter.core_add(k - 1, gt.at[(k - 1) % 2])
            if k - 1 < 2:
                scatter.x_copy(k - 1).start()
    scatter.core_add(3, gt.at[1])
    scatter.c_copy(2, gt.at[0]).wait_send()
    scatter.c_copy(3, gt.at[1]).wait_send()
    for k in range(2):
        up_ref[k] = s1[2 + k]

    def d_copy(c, h):
        part = pl.ds(pl.multiple_of(c * part_rows, part_rows), part_rows)
        return remote(
            dcs.at[h, part, :], do_ref.at[slab, part, :], d_send.at[c, h], d_recv.at[c, slab],
            at.dev(h, at.turned(slab)),
        )

    even = lax.rem(slab, 2) == 0

    def back_two(c, _):
        part = pl.ds(pl.multiple_of(c * part_rows, part_rows), part_rows)
        b_copy(c).wait()
        d_two = bs[c].astype(f32) + br[c].astype(f32)
        normed = normed_s[part, :]
        scaled = d_two * gain_ref[...]
        first = jnp.mean(scaled, axis=-1, keepdims=True)
        second = jnp.mean(scaled * normed, axis=-1, keepdims=True)
        d_hidden = dh_ref[part, :] + inv_s[part, :] * (scaled - first - normed * second)
        vec_ref[0:1, :] += jnp.sum(d_two * normed, axis=0, keepdims=True)
        vec_ref[1:2, :] += jnp.sum(d_two, axis=0, keepdims=True)
        dh_ref[part, :] = d_hidden
        g_attn = d_hidden.astype(bf16)
        gas[part, :] = g_attn
        d_context = nt(g_attn, wo[...]).astype(bf16)
        for h in range(4):
            dcs[h, part, :] = d_context[:, h * HEAD_DIM : (h + 1) * HEAD_DIM]
            home = jnp.logical_and(slab == h, even)

            @pl.when(home)
            def _():
                do_ref[slab, part, :] = dcs[h, part, :]

            @pl.when(jnp.logical_not(home))
            def _():
                d_copy(c, h).start()

        return 0

    lax.fori_loop(0, CHUNKS, back_two, 0)
    go_ref[...] = tn(gas[...], heads_row(ctx_ref, slice(None))).astype(bf16)
    for k in range(2):
        scatter.x_add(k)
        scatter.x_copy(k).wait_send()

    def finish(c, _):
        part = pl.ds(pl.multiple_of(c * part_rows, part_rows), part_rows)
        for h in range(4):
            home = jnp.logical_and(slab == h, even)

            @pl.when(jnp.logical_not(home))
            def _():
                d_copy(c, h).wait_send()
                slot = do_ref.at[h, part, :]
                remote(
                    slot, slot, d_send.at[c, h], d_recv.at[c, h], at.dev(h, seat)
                ).wait_recv()

        return 0

    lax.fori_loop(0, CHUNKS, finish, 0)


def backward_kernel(
    kv_ref, q_ref, ot_ref, ls_ref, do_ref, up_ref, dn_ref,
    dq_ref, dkv_ref, gd_ref, s2_ref,
    grads, acc, delta, near_out, near_in, wide_out, wide_in, home_out, dqs, kept,
    n_send, n_recv, w_send, w_recv, h_send, h_recv, d_send, d_recv,
    rx, ra, s3, rb, up_send, up_recv, dn_send, dn_recv,
):
    at = Place()
    slab, seat = at.slab, at.seat
    core, wide = lax.rem(seat, 2), lax.div(seat, 2)
    rows = q_ref.shape[1]
    per = rows // STEPS
    even = lax.rem(slab, 2) == 0
    ready = greet(at.peers(True, True, True, False))
    up = Scatter(at, None, up_ref, rx, s2_ref, None, None, None, up_send, up_recv)
    down = Scatter(at, None, None, None, dn_ref, ra, s3, rb, dn_send, dn_recv)
    acc[...] = jnp.zeros_like(acc)
    for slot in range(4):
        delta[slot] = jnp.sum(do_ref[slot].astype(f32).T * ot_ref[slot], axis=0, keepdims=True)
    ready()
    for k in range(2):
        down.a_copy(k).start()
        up.x_copy(k).start()

    def unit(slot, t, buf, first, slabs, blocks, allowed):
        size = slabs * blocks * per
        pick = (slice(first, first + slabs), slice(0, blocks))
        keys = kv_ref[(0,) + pick + (t,)].reshape(size, HEAD_DIM)
        values = kv_ref[(1,) + pick + (t,)].reshape(size, HEAD_DIM)
        query = q_ref[slot]
        d_out = do_ref[slot]
        scores = nt(keys, query) * LOG_SCALE - ls_ref[slot]
        if allowed is not None:
            scores = jnp.where(allowed, scores, NEGATIVE)
        prob = jnp.exp2(scores)
        d_probs = nt(values, d_out)
        d_scores = (prob * (d_probs - delta[slot])).astype(bf16)
        shape = (slabs, blocks, per, HEAD_DIM)
        grads[(buf, 1) + pick] += nn(prob.astype(bf16), d_out).reshape(shape)
        grads[(buf, 0) + pick] += nn(d_scores, query).reshape(shape)
        acc[slot] += tn(keys, d_scores)

    def d_copy(slot):
        return remote(
            dqs.at[slot], dq_ref.at[slab], d_send.at[slot], d_recv.at[slab],
            at.dev(slot, at.turned(slot)),
        )

    def slot_step(slot, t, buf):
        if slot > 0:
            unit(slot, t, buf, 0, slot, 4, None)
        mine = at.turned(slot)
        for blocks, chosen in ((2, mine < 2), (4, mine >= 2)):

            @pl.when(chosen)
            def _():
                allowed = attend_mask(blocks * per, rows, per, t, mine)
                unit(slot, t, buf, slot, 1, blocks, allowed)

        @pl.when(t == STEPS - 1)
        def _():
            dqs[slot] = (acc[slot] * HEAD_SCALE).T.astype(bf16)
            home = jnp.logical_and(slab == slot, even)

            @pl.when(home)
            def _():
                dq_ref[slab] = dqs[slot]

            @pl.when(jnp.logical_not(home))
            def _():
                d_copy(slot).start()

    def part(buf, x, c):
        return grads[buf, :, :, 2 * x + c]

    def near_copy(t):
        return remote(
            near_out.at[t], near_in.at[t], n_send.at[t], n_recv.at[t], at.dev(slab, at.core_seat)
        )

    def wide_copy(t):
        return remote(
            wide_out.at[t], wide_in.at[t], w_send.at[t], w_recv.at[t], at.dev(slab, at.x_seat)
        )

    def home_copy(t, k):
        return remote(
            home_out.at[t, :, k], dkv_ref.at[slab, :, t], h_send.at[t, k], h_recv.at[t, slab],
            at.dev(k, seat),
        )

    def near_stage(t, buf):
        near_copy(t).wait_recv()
        wide_out[t] = (part(buf, 1 - wide, core) + near_in[t, 1 - wide].astype(f32)).astype(bf16)
        wide_copy(t).start()
        kept[...] = part(buf, wide, core) + near_in[t, wide].astype(f32)

    def wide_stage(t):
        wide_copy(t).wait_recv()
        home_out[t, 0] = ((kept[0] + wide_in[t, 0].astype(f32)) * HEAD_SCALE).astype(bf16)
        home_out[t, 1] = (kept[1] + wide_in[t, 1].astype(f32)).astype(bf16)
        dkv_ref[slab, :, t] = home_out[t, :, slab]
        for step in range(1, 4):
            home_copy(t, lax.rem(slab + step, 4)).start()

    def go(t, _):
        buf = lax.rem(t, 2)
        grads[buf] = jnp.zeros_like(grads[buf])
        slot_step(3, t, buf)

        @pl.when(t > 0)
        def _():
            near_stage(t - 1, 1 - buf)

        slot_step(0, t, buf)
        slot_step(2, t, buf)

        @pl.when(t > 0)
        def _():
            wide_stage(t - 1)

        slot_step(1, t, buf)
        for x in range(2):
            near_out[t, x] = part(buf, x, 1 - core).astype(bf16)
        near_copy(t).start()
        for k in range(2):

            @pl.when(t == k + 1)
            def _():
                down.a_add(k)
                down.b_copy(k).start()

        return 0

    lax.fori_loop(0, STEPS, go, 0)
    near_stage(STEPS - 1, (STEPS - 1) % 2)
    half = gd_ref.shape[0] // 2
    for k in range(2):
        up.x_add(k)
        gd_ref[k * half : (k + 1) * half, :] = down.b_add(k).T
    wide_stage(STEPS - 1)
    for k in range(2):
        down.a_copy(k).wait_send()
        down.b_copy(k).wait_send()
        up.x_copy(k).wait_send()

    def finish(t, _):
        near_copy(t).wait_send()
        wide_copy(t).wait_send()
        for step in range(1, 4):
            k = lax.rem(slab + step, 4)
            home_copy(t, k).wait_send()
            slot = dkv_ref.at[k, :, t]
            remote(slot, slot, h_send.at[t, k], h_recv.at[t, k], at.dev(k, seat)).wait_recv()
        return 0

    lax.fori_loop(0, STEPS, finish, 0)
    for k in range(4):
        home = jnp.logical_and(slab == k, even)

        @pl.when(jnp.logical_not(home))
        def _():
            d_copy(k).wait_send()
            slot = dq_ref.at[k]
            remote(slot, slot, d_send.at[k], d_recv.at[k], at.dev(k, seat)).wait_recv()


def tail_kernel(
    dq_ref, dkv_ref, n_one_ref, wq_ref, wk_ref, wv_ref, x_ref, gain_ref, dh_ref, vec_ref, go_ref,
    cnt_ref, up_ref,
    ig_ref, gq_ref, gk_ref, gv_ref, go_out, gu_ref, g1_ref, b1_ref, g2_ref, b2_ref, loss_ref,
    vsum_ref,
    ga, rc, s1, rx, s2, ra, s3, rb, g_send, g_recv, ua, u3, ub, u_send, u_recv, bs, br, dcat,
    b_send, b_recv,
    tile, core_in, x_buf, x_in, z_buf, z_in, t_send, t_recv,
):
    at = Place()
    rows = x_ref.shape[0]
    part_rows = rows // CHUNKS
    ready = greet(at.peers(True, False, True, True))
    scatter = Scatter(at, rc, s1, rx, s2, ra, s3, rb, g_send, g_recv)
    up = Scatter(at, None, None, None, up_ref, ua, u3, ub, u_send, u_recv)

    def b_copy(c):
        return remote(bs.at[c], br.at[c], b_send.at[c], b_recv.at[c], at.other_side())

    dcat[0] = heads_row(dq_ref, slice(None))
    for j in range(2):
        dcat[1 + j] = jnp.concatenate([dkv_ref[h, j] for h in range(4)], axis=1)
    ready()
    scatter.c_copy(0, go_ref).start()
    for k in range(2):
        up.a_copy(k).start()

    def side_part(c, _):
        part = pl.ds(pl.multiple_of(c * part_rows, part_rows), part_rows)
        bs[c] = (
            nt(dcat[0, part, :], wq_ref[...])
            + nt(dcat[1, part, :], wk_ref[...])
            + nt(dcat[2, part, :], wv_ref[...])
        ).astype(bf16)
        b_copy(c).start()
        return 0

    lax.fori_loop(0, CHUNKS, side_part, 0)
    scatter.core_add(0, go_ref)
    scatter.x_copy(0).start()
    for j in range(3):
        ga[j] = tn(n_one_ref[...], dcat[j]).astype(bf16).reshape(ga.shape[1:])
        scatter.c_copy(j + 1, ga.at[j]).start()
        if j > 0:
            scatter.core_add(j, ga.at[j - 1])
            scatter.x_copy(j).start()
    scatter.core_add(3, ga.at[2])
    scatter.x_copy(3).start()
    for k in range(2):
        up.a_add(k)
        up.b_copy(k).start()
    tile[...] = vec_ref[...]
    tile[3:5, :] = jnp.zeros_like(tile[3:5, :])
    scatter.x_add(0)
    scatter.a_copy(0).start()

    def side_sum(c, _):
        part = pl.ds(pl.multiple_of(c * part_rows, part_rows), part_rows)
        b_copy(c).wait()
        d_one = bs[c].astype(f32) + br[c].astype(f32)
        normed, inverse = norm_stats(x_ref[part, :])
        scaled = d_one * gain_ref[...]
        first = jnp.mean(scaled, axis=-1, keepdims=True)
        second = jnp.mean(scaled * normed, axis=-1, keepdims=True)
        ig_ref[part, :] = dh_ref[part, :] + inverse * (scaled - first - normed * second)
        tile[3:4, :] += jnp.sum(d_one * normed, axis=0, keepdims=True)
        tile[4:5, :] += jnp.sum(d_one, axis=0, keepdims=True)
        for k in range(1, 4):

            @pl.when(c == k)
            def _():
                scatter.x_add(k)
                scatter.a_copy(k).start()
                scatter.a_add(k - 1)
                scatter.b_copy(k - 1).start()

        return 0

    lax.fori_loop(0, CHUNKS, side_sum, 0)
    total = Summed(at, tile, core_in, x_buf, x_in, z_buf, z_in, t_send, t_recv)
    total.one()
    half = gu_ref.shape[1] // 2
    for k in range(2):
        gu_ref[:, k * half : (k + 1) * half] = up.b_add(k)
    total.two()
    scatter.a_add(3)
    scatter.b_copy(3).start()
    go_out[...] = scatter.b_add(0).T
    total.three()
    gq_ref[...] = scatter.b_add(1)
    gk_ref[...] = scatter.b_add(2)
    gv_ref[...] = scatter.b_add(3)
    vsum_ref[...] = total.four()
    share = gq_ref.shape[0]
    for k in range(SEQ_DEV):

        @pl.when(at.pos == k)
        def _():
            for line, ref in ((3, g1_ref), (4, b1_ref), (0, g2_ref), (1, b2_ref)):
                ref[...] = vsum_ref[line : line + 1, k * share : (k + 1) * share]

    loss_ref[...] = jnp.sum(vsum_ref[2:3, :], axis=1, keepdims=True) / (2.0 * cnt_ref[0:1, 0:1])
    for k in range(4):
        scatter.c_copy(k, go_ref if k == 0 else ga.at[k - 1]).wait_send()
        scatter.x_copy(k).wait_send()
        scatter.a_copy(k).wait_send()
        scatter.b_copy(k).wait_send()
    for k in range(2):
        up.a_copy(k).wait_send()
        up.b_copy(k).wait_send()


def in_vmem():
    return pl.BlockSpec(memory_space=pltpu.VMEM)


def in_hbm():
    return pl.BlockSpec(memory_space=pl.ANY)


def dma(*shape):
    return pltpu.SemaphoreType.DMA(shape)


def call(kernel, name, ident, outs, ins, scratch, args, flops=0):
    return pl.pallas_call(
        kernel,
        name=name,
        out_shape=outs,
        in_specs=ins,
        out_specs=tuple(in_vmem() for _ in outs),
        scratch_shapes=scratch,
        compiler_params=pltpu.CompilerParams(
            collective_id=ident, has_side_effects=True, vmem_limit_bytes=62 * 2**20
        ),
        cost_estimate=pl.CostEstimate(flops=flops, bytes_accessed=2**24, transcendentals=0),
    )(*args)


def per_device(
    inputs, ln1_gain, ln1_bias, w_query, w_key, w_value, w_out, ln2_gain, ln2_bias, w_up, w_down,
    teacher, valid_mask,
):
    rows, width = inputs.shape
    local = w_query.shape[1]
    heads = local // HEAD_DIM
    hidden_units = w_up.shape[1]
    dp_size = lax.axis_size("dp")
    single = dp_size == SEQ_DEV
    share = width // SEQ_DEV
    out = jax.ShapeDtypeStruct
    row = lambda vector: vector.reshape(1, width)
    step_rows = rows // STEPS
    part_rows = rows // CHUNKS

    n_one, kv_all, q_all, o_t, log_sum, ctx, count, wo_in = call(
        forward_kernel, "forward", 1,
        (
            out((rows, width), bf16),
            out((2, 4, 4, STEPS, step_rows, HEAD_DIM), bf16),
            out((4, rows, HEAD_DIM), bf16),
            out((4, HEAD_DIM, rows), f32),
            out((4, 1, rows), f32),
            out((heads, rows, HEAD_DIM), bf16),
            out((8, 128), f32),
            out((local, width), bf16),
        ),
        [in_vmem()] * 8,
        [
            pltpu.VMEM((heads, 2, STEPS, step_rows, HEAD_DIM), bf16),
            pltpu.VMEM((heads, rows, HEAD_DIM), bf16),
            pltpu.VMEM((4, rows, HEAD_DIM), bf16),
            pltpu.VMEM((4, 1, rows), f32),
            pltpu.VMEM((4, 1, rows), f32),
            dma(STEPS, 4), dma(STEPS, 4), dma(4), dma(4),
        ]
        + [dma(STEPS)] * 6
        + [dma(4)] * 2
        + [dma(2)]
        + summed_scratch((8, 128)),
        (
            inputs, row(ln1_gain), row(ln1_bias), w_query, w_key, w_value, w_out,
            valid_mask.reshape(1, rows),
        ),
    )
    if not single:
        count = jnp.full((8, 128), lax.psum(jnp.sum(valid_mask.astype(f32)), "dp"))
    share = width // SEQ_DEV
    split = (4, 2, 2, share)
    piece = hidden_units // 2
    output, d_hidden, do_all, up_part, down_part, grad_out_t, vectors = call(
        functools.partial(middle_kernel, float(rows * dp_size)), "middle", 2,
        (
            out((rows, width), f32),
            out((rows, width), f32),
            out((4, rows, HEAD_DIM), bf16),
            out((2, 4, 2, share, piece), bf16),
            out((2, 2, 2, share, piece), bf16),
            out((width, local), bf16),
            out((8, width), f32),
        ),
        [
            in_vmem(), in_hbm(), in_hbm(), in_hbm(), in_vmem(), in_vmem(), in_hbm(), in_hbm(),
            in_hbm(), in_vmem(), in_vmem(),
        ],
        [
            pltpu.VMEM((rows, width), f32),
            pltpu.VMEM((local, width), bf16),
            pltpu.VMEM((local, width), bf16),
            pltpu.VMEM((width, hidden_units), bf16),
            pltpu.VMEM((hidden_units, width), bf16),
            pltpu.VMEM((rows, width), f32),
            dma(6),
            pltpu.VMEM((heads, rows, HEAD_DIM), bf16),
            pltpu.VMEM((rows, width), f32),
            pltpu.VMEM((rows, 1), f32),
            pltpu.VMEM((rows, width), bf16),
            pltpu.VMEM((rows, hidden_units), bf16),
            pltpu.VMEM((rows, width), bf16),
            pltpu.VMEM((rows, hidden_units), bf16),
            pltpu.VMEM((rows, width), bf16),
            pltpu.VMEM((heads, rows, HEAD_DIM), bf16),
        ]
        + [pltpu.VMEM((CHUNKS, part_rows, width), bf16)] * 4
        + [dma(CHUNKS)] * 6
        + [dma(CHUNKS, 4)] * 2
        + [
            pltpu.VMEM((2,) + split + (piece,), bf16),
            pltpu.VMEM((4, 4, 2, share, piece), bf16),
            pltpu.VMEM((4, 4, 2, share, piece), bf16),
            pltpu.VMEM((2, 4, share, piece), bf16),
            dma(2, 4), dma(2, 4),
        ],
        (
            ctx, inputs, w_out, wo_in, row(ln2_gain), row(ln2_bias), w_up, w_down, teacher,
            valid_mask.astype(f32).reshape(rows, 1), count,
        ),
    )
    d_query, d_kv, grad_down, up_part = call(
        backward_kernel, "backward", 3,
        (
            out((heads, rows, HEAD_DIM), bf16),
            out((heads, 2, STEPS, step_rows, HEAD_DIM), bf16),
            out((hidden_units, share), f32),
            out((2, 2, 2, share, piece), bf16),
        ),
        [in_vmem()] * 7,
        [
            pltpu.VMEM((2, 2, 4, 4, step_rows, HEAD_DIM), f32),
            pltpu.VMEM((4, HEAD_DIM, rows), f32),
            pltpu.VMEM((4, 1, rows), f32),
            pltpu.VMEM((STEPS, 2, 2, 4, step_rows, HEAD_DIM), bf16),
            pltpu.VMEM((STEPS, 2, 2, 4, step_rows, HEAD_DIM), bf16),
            pltpu.VMEM((STEPS, 2, 4, step_rows, HEAD_DIM), bf16),
            pltpu.VMEM((STEPS, 2, 4, step_rows, HEAD_DIM), bf16),
            pltpu.VMEM((STEPS, 2, 4, step_rows, HEAD_DIM), bf16),
            pltpu.VMEM((4, rows, HEAD_DIM), bf16),
            pltpu.VMEM((2, 4, step_rows, HEAD_DIM), f32),
            dma(STEPS), dma(STEPS), dma(STEPS), dma(STEPS), dma(STEPS, 4), dma(STEPS, 4),
            dma(4), dma(4),
            pltpu.VMEM((2, 4, share, piece), bf16),
            pltpu.VMEM((2, 2, share, piece), bf16),
            pltpu.VMEM((2, 2, share, piece), bf16),
            pltpu.VMEM((2, share, piece), bf16),
            dma(4, 2), dma(4, 2), dma(4, 2), dma(4, 2),
        ],
        (kv_all, q_all, o_t, log_sum, do_all, up_part, down_part),
    )
    (
        input_grad, grad_query, grad_key, grad_value, grad_out, grad_up, gain_one, bias_one,
        gain_two, bias_two, loss, sums,
    ) = call(
        tail_kernel, "tail", 4,
        (out((rows, width), f32),)
        + (out((share, local), f32),) * 3
        + (out((local, share), f32), out((share, hidden_units), f32))
        + (out((1, share), f32),) * 4
        + (out((1, 1), f32), out((8, width), f32)),
        [in_vmem()] * 13,
        [
            pltpu.VMEM((3,) + split + (local,), bf16),
            pltpu.VMEM((4, 4, 2, share, local), bf16),
            pltpu.VMEM((4, 4, 2, share, local), bf16),
            pltpu.VMEM((4, 4, share, local), bf16),
            pltpu.VMEM((4, 2, 2, share, local), bf16),
            pltpu.VMEM((4, 2, share, local), bf16),
            pltpu.VMEM((4, 2, share, local), bf16),
            pltpu.VMEM((4, share, local), bf16),
            dma(4, 4), dma(4, 4),
            pltpu.VMEM((2, 2, share, piece), bf16),
            pltpu.VMEM((2, 2, share, piece), bf16),
            pltpu.VMEM((2, share, piece), bf16),
            dma(4, 2), dma(4, 2),
            pltpu.VMEM((CHUNKS, part_rows, width), bf16),
            pltpu.VMEM((CHUNKS, part_rows, width), bf16),
            pltpu.VMEM((3, rows, local), bf16),
            dma(CHUNKS), dma(CHUNKS),
        ]
        + summed_scratch((8, width)),
        (
            d_query, d_kv.reshape(heads, 2, rows, HEAD_DIM), n_one, w_query, w_key, w_value,
            inputs, row(ln1_gain), d_hidden, vectors, grad_out_t.reshape(split + (local,)), count,
            up_part,
        ),
    )
    small = [gain_one, bias_one, gain_two, bias_two]
    small = [vector.reshape(share) for vector in small]
    loss_value = loss.reshape(())
    if not single:
        index = lax.axis_index("dp")
        first = lax.rem(index, SEQ_DEV) * share

        def spread(part, axis):
            shape = list(part.shape)
            shape[axis] = width
            at = [0, 0]
            at[axis] = first
            placed = lax.dynamic_update_slice(jnp.zeros(shape, f32), part, tuple(at))
            return lax.psum_scatter(placed, "dp", scatter_dimension=axis, tiled=True)

        grad_query, grad_key, grad_value, grad_up = (
            spread(part, 0) for part in (grad_query, grad_key, grad_value, grad_up)
        )
        grad_out, grad_down = spread(grad_out, 1), spread(grad_down, 1)
        sums = lax.psum(jnp.where(first == 0, sums, 0.0), "dp")
        length = width // dp_size
        small = [lax.dynamic_slice(sums[k], (index * length,), (length,)) for k in (3, 4, 0, 1)]
        loss_value = jnp.sum(sums[2]) / (2.0 * count[0, 0])
    return (
        output, loss_value, input_grad, small[0], small[1], grad_query, grad_key, grad_value,
        grad_out, small[2], small[3], grad_up, grad_down,
    )


def solution(mesh):
    return jax.shard_map(
        per_device,
        mesh=mesh,
        in_specs=(
            P("dp", None), P(), P(), P(None, "tensor"), P(None, "tensor"), P(None, "tensor"),
            P("tensor", None), P(), P(), P(None, "tensor"), P("tensor", None), P("dp", None),
            P("dp"),
        ),
        out_specs=(
            P("dp", None), P(), P("dp", None), P("dp"), P("dp"), P("dp", "tensor"),
            P("dp", "tensor"), P("dp", "tensor"), P("tensor", "dp"), P("dp"), P("dp"),
            P("dp", "tensor"), P("tensor", "dp"),
        ),
        check_vma=False,
    )
```

time: 405 us -> 318 us (0.79)
  Pallas kernels: 390 us -> 301 us
  local copies, waits for them, and re-layouts: 9.13 us -> 13.2 us
    pallas_call x4, Pallas kernels: 390 us -> 301 us  [call(): pl.pallas_call(kernel, name=name, out_shape=outs, in_specs=ins, out_specs...]
    unnamed x10 -> x32, local copies, waits for them, and re-layouts: 3.67 us -> 12.3 us
where the time goes in v2:
time: 318 us; the launch traced here: 317 us
  Pallas kernels  301 us (95%)
  local copies, waits for them, and re-layouts  13.2 us (4%)
    pallas_call x4, Pallas kernels, call(): pl.pallas_call(kernel, name=name, out_shape=outs, in_specs=ins, out_specs...  301 us
    unnamed x32, local copies, waits for them, and re-layouts  12.3 us

profile of v2, /device:TPU:0, one launch (start us, length us, event | category | flops | bytes accessed | tf_op | source)
XLA Modules:
  0.0 317.4 jit_solution(12417677280837937283)
XLA Ops:
  0.6 0.7 convert_element_type.3
  1.3 0.9 copy.28.mask_ref
  2.2 80.3 %forward.1 = (bf16[512,1024]{1,0:T(8,128)(2,1)}, bf16[2,4,4,4,128,128]{5,4,3,2,1,0:T(8,128)(2,1)}, bf16[4,512,128]{2,1,0:T(8,128)(2,1)}, f32[4,128,512]{2,1,0:T(...) custom-call(f32[512,1024]{1,0:T(8,128)} %x_ref.3, ...), custom_call_target="tpu_custom_call" | custom-call | bytes 16777216 | tf_op jit(solution)/shard_map/forward/pallas_call | solution.py:940
  82.5 83.8 %middle.1 = (f32[512,1024]{1,0:T(8,128)}, f32[512,1024]{1,0:T(8,128)}, bf16[4,512,128]{2,1,0:T(8,128)(2,1)}, bf16[2,4,2,64,1024]{4,3,2,1,0:T(8,128)(2,1)}, bf16[...) custom-call(bf16[4,512,128]{2,1,0:T(8,128)(2,1)} %get-tuple-element.43.ctx_ref, ...), custom_call_target="tpu_custom_call" | custom-call | bytes 16777216 | tf_op jit(solution)/shard_map/middle/pallas_call | solution.py:940
  166.3 87.9 %backward.1 = (bf16[4,512,128]{2,1,0:T(8,128)(2,1)}, bf16[4,2,4,128,128]{4,3,2,1,0:T(8,128)(2,1)}, f32[2048,64]{1,0:T(8,128)}, bf16[2,2,2,64,1024]{4,3,2,1,0:T(8,128)(2,1)}) custom-call(bf16[2,4,4,4,128,128]{5,4,3,2,1,0:T(8,128)(2,1)} %get-tuple-element.47.kv_ref, bf16[4,512,128]{2,1,0:T(8,128)(2,1)} %get-tuple-element.48.q_ref, ...), custom_call_target="tpu_custom_call" | custom-call | bytes 16777216 | tf_op jit(solution)/shard_map/backward/pallas_call | solution.py:940
  254.2 0.0 copy-start.1
  254.2 49.0 %tail.1 = (f32[512,1024]{1,0:T(8,128)}, f32[64,512]{1,0:T(8,128)}, f32[64,512]{1,0:T(8,128)}, f32[64,512]{1,0:T(8,128)}, f32[512,64]{1,0:T(8,128)}, /*index=5*/f...) custom-call(bf16[4,512,128]{2,1,0:T(8,128)(2,1)} %get-tuple-element., ...), custom_call_target="tpu_custom_call" | custom-call | bytes 16777216 | tf_op jit(solution)/shard_map/tail/pallas_call | solution.py:940
  303.3 1.7 copy.29
  305.0 0.0 copy-done.1
  305.0 1.1 copy.30
  306.1 0.0 copy-start
  306.1 3.3 %copy.42 = f32[512,1024]{1,0:T(8,128)} copy(f32[512,1024]{1,0:T(8,128)} %get-tuple-element.112) | data formatting | bytes 4194304
  310.0 0.0 copy-done
  310.0 0.0 copy-start.9
  310.1 0.0 copy-start.8
  310.1 0.0 copy-start.5
  310.1 0.0 copy-start.4
  310.1 0.0 copy-start.3
  310.1 0.0 copy-start.7
  310.1 0.0 copy-start.6
  310.1 0.0 copy-start.2
  310.1 1.3 copy.44
  311.4 0.0 copy-done.9
  311.4 0.5 copy.45
  312.0 0.0 copy-done.8
  312.0 0.5 copy.46
  312.5 0.0 copy-done.5
  312.5 0.7 copy.47
  313.1 0.0 copy-done.4
  313.1 0.7 copy.48
  313.8 0.0 copy-done.3
  313.8 0.7 copy.49
  314.4 0.0 copy-done.7
  314.5 0.5 copy.50
  315.0 0.0 copy-done.6
  315.0 0.5 copy.51
  315.5 0.0 copy-done.2
  315.5 0.8 copy.52
Async XLA Ops:
  254.2 50.8 %copy-start.1 = (f32[2048,64]{1,0:T(8,128)S(1)}, f32[2048,64]{1,0:T(8,128)}, u32[]{:S(2)}) copy-start(f32[2048,64]{1,0:T(8,128)} %get-tuple-element.98) | copy-start | bytes 1572868
  306.1 3.9 %copy-start = (f32[512,1024]{1,0:T(8,128)S(1)}, f32[512,1024]{1,0:T(8,128)}, u32[]{:S(2)}) copy-start(f32[512,1024]{1,0:T(8,128)} %get-tuple-element.114) | copy-start | bytes 6291460
  310.0 1.4 copy-start.9
  310.1 1.9 copy-start.8
  310.1 2.4 copy-start.5
  310.1 3.1 copy-start.4
  310.1 3.7 %copy-start.3 = (f32[64,512]{1,0:T(8,128)S(1)}, f32[64,512]{1,0:T(8,128)}, u32[]{:S(2)}) copy-start(f32[64,512]{1,0:T(8,128)} %get-tuple-element.119) | copy-start | bytes 393220
  310.1 4.4 %copy-start.7 = (f32[1,64]{1,0:T(1,128)S(1)}, f32[1,64]{1,0:T(1,128)}, u32[]{:S(2)}) copy-start(f32[1,64]{1,0:T(1,128)} %get-tuple-element.69) | copy-start | bytes 772
  310.1 4.9 %copy-start.6 = (f32[1,64]{1,0:T(1,128)S(1)}, f32[1,64]{1,0:T(1,128)}, u32[]{:S(2)}) copy-start(f32[1,64]{1,0:T(1,128)} %get-tuple-element.70) | copy-start | bytes 772
  310.1 5.4 %copy-start.2 = (f32[64,2048]{1,0:T(8,128)S(1)}, f32[64,2048]{1,0:T(8,128)}, u32[]{:S(2)}) copy-start(f32[64,2048]{1,0:T(8,128)} %get-tuple-element.123) | copy-start | bytes 1572868

commit v3 on v2

--- a/solution.py
+++ b/solution.py
@@ -15,6 +15,7 @@
 HEAD_SCALE = HEAD_DIM ** (-0.5)
 CHUNKS = 4
 STEPS = 4
+FSTEPS = 4
 f32 = jnp.float32
 bf16 = jnp.bfloat16
 
@@ -234,15 +235,15 @@
 
 def forward_kernel(
     x_ref, gain_ref, bias_ref, wq_ref, wk_ref, wv_ref, wo_ref, mask_ref,
-    none_ref, kv_ref, q_ref, ot_ref, ls_ref, ctx_ref, cnt_ref, wo_in_ref,
+    none_ref, kv_ref, q_ref, ot_ref, ls_ref, ctx_ref, ctx_in_ref, cnt_ref, wo_in_ref,
     kvs, qs, os, top, low,
     z_send, z_recv, q_send, q_recv, c_send, c_recv, x_send, x_recv, f_send, f_recv,
-    o_send, o_recv, w_sem,
+    o_send, o_recv, e_send, e_recv, w_sem,
     tile, core_in, x_buf, x_in, z_buf, z_in, t_send, t_recv,
 ):
     at = Place()
     rows = x_ref.shape[0]
-    per = rows // STEPS
+    per = rows // FSTEPS
     slab, seat = at.slab, at.seat
     even = lax.rem(slab, 2) == 0
     odd = jnp.logical_not(even)
@@ -296,8 +297,8 @@
     for j, w_ref in enumerate((wk_ref, wv_ref)):
         made = nn(none_ref[...], w_ref[...]).astype(bf16)
         for h in range(4):
-            kvs[h, j] = made[:, h * HEAD_DIM : (h + 1) * HEAD_DIM].reshape(STEPS, per, HEAD_DIM)
-    for t in range(STEPS):
+            kvs[h, j] = made[:, h * HEAD_DIM : (h + 1) * HEAD_DIM].reshape(FSTEPS, per, HEAD_DIM)
+    for t in range(FSTEPS):
         for k in range(3):
             kv_copy(order(k), t).start()
     kv_ref[:, slab, seat] = kvs[slab]
@@ -333,17 +334,25 @@
         part = kv_ref.at[:, :, at.far_seat, t]
         remote(part, part, f_send.at[t], f_recv.at[t], device).wait_recv()
 
-    def unit(slot, keys, values, allowed):
-        scores = nt(keys, q_ref[slot]) * LOG_SCALE
-        if allowed is not None:
-            scores = jnp.where(allowed, scores, NEGATIVE)
-        before = top[slot]
-        after = jnp.maximum(before, jnp.max(scores, axis=0, keepdims=True))
-        prob = jnp.exp2(scores - after)
+    def unit(slot, parts):
+        scored = []
+        after = before = top[slot]
+        for keys, _, allowed in parts:
+            scores = nt(keys, q_ref[slot]) * LOG_SCALE
+            if allowed is not None:
+                scores = jnp.where(allowed, scores, NEGATIVE)
+            after = jnp.maximum(after, jnp.max(scores, axis=0, keepdims=True))
+            scored.append(scores)
         shrink = jnp.exp2(before - after)
-        low[slot] = low[slot] * shrink + jnp.sum(prob, axis=0, keepdims=True)
+        total_low = low[slot] * shrink
+        total = ot_ref[slot] * shrink
+        for scores, (_, values, _) in zip(scored, parts):
+            prob = jnp.exp2(scores - after)
+            total_low = total_low + jnp.sum(prob, axis=0, keepdims=True)
+            total = total + tn(values, prob.astype(bf16))
+        low[slot] = total_low
         top[slot] = after
-        ot_ref[slot] = ot_ref[slot] * shrink + tn(values, prob.astype(bf16))
+        ot_ref[slot] = total
 
     def o_copy(slot):
         return remote(
@@ -352,28 +361,26 @@
         )
 
     def slot_step(slot, t):
-        if slot > 0:
-            size = 4 * slot * per
-            unit(
-                slot,
-                kv_ref[0, 0:slot, :, t].reshape(size, HEAD_DIM),
-                kv_ref[1, 0:slot, :, t].reshape(size, HEAD_DIM),
-                None,
-            )
         mine = at.turned(slot)
+
+        def taken(pick, size, allowed):
+            keys = kv_ref[(0,) + pick + (t,)].reshape(size, HEAD_DIM)
+            values = kv_ref[(1,) + pick + (t,)].reshape(size, HEAD_DIM)
+            return keys, values, allowed
+
         for blocks, chosen in ((2, mine < 2), (4, mine >= 2)):
 
             @pl.when(chosen)
             def _():
+                parts = []
+                if slot > 0:
+                    parts.append(taken((slice(0, slot), slice(0, 4)), 4 * slot * per, None))
                 size = blocks * per
-                unit(
-                    slot,
-                    kv_ref[0, slot, 0:blocks, t].reshape(size, HEAD_DIM),
-                    kv_ref[1, slot, 0:blocks, t].reshape(size, HEAD_DIM),
-                    attend_mask(size, rows, per, t, mine),
-                )
-
-        @pl.when(t == STEPS - 1)
+                allowed = attend_mask(size, rows, per, t, mine)
+                parts.append(taken((slot, slice(0, blocks)), size, allowed))
+                unit(slot, parts)
+
+        @pl.when(t == FSTEPS - 1)
         def _():
             done = ot_ref[slot] / low[slot]
             ot_ref[slot] = done
@@ -410,13 +417,9 @@
         arrive(t)
         slot_step(3, t)
 
-        @pl.when(t + 2 < STEPS)
+        @pl.when(t + 2 < FSTEPS)
         def _():
             relay(t + 2)
-
-        @pl.when(t + 1 < STEPS)
-        def _():
-            hand_on(t + 1)
 
         @pl.when(t == 0)
         def _():
@@ -424,10 +427,15 @@
 
         slot_step(0, t)
         slot_step(2, t)
+
+        @pl.when(t + 1 < FSTEPS)
+        def _():
+            hand_on(t + 1)
+
         slot_step(1, t)
         return 0
 
-    lax.fori_loop(0, STEPS, go, 0)
+    lax.fori_loop(0, FSTEPS, go, 0)
     cnt_ref[...] = total.four()
     for k in range(3):
         q_copy(order(k)).wait_send()
@@ -444,7 +452,20 @@
         pass_copy(t).wait_send()
         return 0
 
-    lax.fori_loop(0, STEPS, finish, 0)
+    def e_copy(k):
+        return remote(ctx_ref.at[k], ctx_in_ref.at[k], e_send.at[k], e_recv.at[k], at.other_side())
+
+    for step in range(4):
+        k = lax.rem(slab + step, 4)
+        home = jnp.logical_and(step == 0, even)
+
+        @pl.when(jnp.logical_not(home))
+        def _():
+            part = ctx_ref.at[k]
+            remote(part, part, o_send.at[k], o_recv.at[k], at.dev(k, seat)).wait_recv()
+
+        e_copy(k).start()
+    lax.fori_loop(0, FSTEPS, finish, 0)
     w_copy.wait()
     for k in range(4):
         home = jnp.logical_and(slab == k, even)
@@ -452,8 +473,8 @@
         @pl.when(jnp.logical_not(home))
         def _():
             o_copy(k).wait_send()
-            part = ctx_ref.at[k]
-            remote(part, part, o_send.at[k], o_recv.at[k], at.dev(k, seat)).wait_recv()
+
+        e_copy(k).wait()
 
 
 def heads_row(ref, rows_at):
@@ -462,13 +483,13 @@
 
 def middle_kernel(
     token_total,
-    ctx_ref, x_hbm, wo_hbm, wo_in_hbm, gain_ref, bias_ref, wup_hbm, wdn_hbm, teach_hbm,
+    ctx_ref, ctx_in, x_hbm, wo_hbm, wo_in_hbm, gain_ref, bias_ref, wup_hbm, wdn_hbm, teach_hbm,
     mask_ref, cnt_ref,
-    out_ref, dh_ref, do_ref, up_ref, dn_ref, go_ref, vec_ref,
+    out_ref, dh_ref, do_ref, one_ref, two_ref, go_ref, vec_ref,
     x_buf, wo, wo_in, wup, wdn, teach, load,
-    ctx_in, normed_s, inv_s, n2s, acts, gfs, dpres, gas, dcs,
+    normed_s, inv_s, n2s, acts, gfs, dpres, gas, dcs,
     fs, fr, bs, br,
-    e_send, e_recv, f_send, f_recv, b_send, b_recv, d_send, d_recv,
+    f_send, f_recv, b_send, b_recv, d_send, d_recv,
     gt, rc, s1, rx, g_send, g_recv,
 ):
     at = Place()
@@ -489,27 +510,17 @@
         copy.start()
     ready()
 
-    def e_copy(c):
-        part = pl.ds(pl.multiple_of(c * part_rows, part_rows), part_rows)
-        return remote(
-            ctx_ref.at[:, part, :], ctx_in.at[:, part, :], e_send.at[c], e_recv.at[c],
-            at.other_side(),
-        )
-
     def f_copy(c):
         return remote(fs.at[c], fr.at[c], f_send.at[c], f_recv.at[c], at.other_side())
 
     def b_copy(c):
         return remote(bs.at[c], br.at[c], b_send.at[c], b_recv.at[c], at.other_side())
 
-    for c in range(CHUNKS):
-        e_copy(c).start()
     for k in range(3):
         loads[k].wait()
 
     def forward(c, _):
         part = pl.ds(pl.multiple_of(c * part_rows, part_rows), part_rows)
-        e_copy(c).wait()
         hidden = x_buf[part, :] + (
             nn(heads_row(ctx_ref, part), wo[...]) + nn(heads_row(ctx_in, part), wo_in[...])
         )
@@ -556,7 +567,7 @@
         return 0
 
     lax.fori_loop(0, CHUNKS, back_one, 0)
-    scatter = Scatter(at, rc, s1, rx, dn_ref, None, None, None, g_send, g_recv)
+    scatter = Scatter(at, rc, s1, rx, two_ref, None, None, None, g_send, g_recv)
     split = gt.shape[1:5]
     half = gt.shape[5] // 2
     for k in range(4):
@@ -575,13 +586,13 @@
         scatter.c_copy(k, slot).start()
         if k >= 1:
             scatter.core_add(k - 1, gt.at[(k - 1) % 2])
-            if k - 1 < 2:
-                scatter.x_copy(k - 1).start()
+            if k == 1:
+                scatter.x_copy(0).start()
     scatter.core_add(3, gt.at[1])
     scatter.c_copy(2, gt.at[0]).wait_send()
     scatter.c_copy(3, gt.at[1]).wait_send()
-    for k in range(2):
-        up_ref[k] = s1[2 + k]
+    for k in range(3):
+        one_ref[k] = s1[1 + k]
 
     def d_copy(c, h):
         part = pl.ds(pl.multiple_of(c * part_rows, part_rows), part_rows)
@@ -623,9 +634,8 @@
 
     lax.fori_loop(0, CHUNKS, back_two, 0)
     go_ref[...] = tn(gas[...], heads_row(ctx_ref, slice(None))).astype(bf16)
-    for k in range(2):
-        scatter.x_add(k)
-        scatter.x_copy(k).wait_send()
+    scatter.x_add(0)
+    scatter.x_copy(0).wait_send()
 
     def finish(c, _):
         part = pl.ds(pl.multiple_of(c * part_rows, part_rows), part_rows)
@@ -646,282 +656,348 @@
 
 
 def backward_kernel(
-    kv_ref, q_ref, ot_ref, ls_ref, do_ref, up_ref, dn_ref,
-    dq_ref, dkv_ref, gd_ref, s2_ref,
-    grads, acc, delta, near_out, near_in, wide_out, wide_in, home_out, dqs, kept,
+    kv_ref, q_ref, ot_ref, ls_ref, do_ref, part_one, part_two, go_ref,
+    n_one_hbm, wq_hbm, wk_hbm, wv_hbm, x_hbm, dh_hbm, gain_ref, vec_ref, cnt_ref,
+    ig_ref, gq_ref, gk_ref, gv_ref, go_out, gu_ref, gd_ref, g1_ref, b1_ref, g2_ref, b2_ref,
+    loss_ref, vsum_ref,
+    dq_ref, dkv_ref, acc, delta, near_out, near_in, wide_out, wide_in, home_out, dqs,
     n_send, n_recv, w_send, w_recv, h_send, h_recv, d_send, d_recv,
-    rx, ra, s3, rb, up_send, up_recv, dn_send, dn_recv,
+    a_one, s3_one, b_one, one_send, one_recv,
+    rx, s2, ra, s3, rb, two_send, two_recv,
+    gc, g1, gx, g2, gg, g3, gb, g_send, g_recv, bs, br,
+    b_send, b_recv, load,
+    tile, core_in, x_buf, x_in, z_buf, z_in, t_send, t_recv,
 ):
     at = Place()
     slab, seat = at.slab, at.seat
     core, wide = lax.rem(seat, 2), lax.div(seat, 2)
     rows = q_ref.shape[1]
     per = rows // STEPS
+    part_rows = rows // CHUNKS
     even = lax.rem(slab, 2) == 0
-    ready = greet(at.peers(True, True, True, False))
-    up = Scatter(at, None, up_ref, rx, s2_ref, None, None, None, up_send, up_recv)
-    down = Scatter(at, None, None, None, dn_ref, ra, s3, rb, dn_send, dn_recv)
+    ready = greet(at.peers(True, True, True, True))
+    first = Scatter(at, None, None, None, part_two, a_one, s3_one, b_one, one_send, one_recv)
+    rest = Scatter(at, None, part_one, rx, s2, ra, s3, rb, two_send, two_recv)
+    own = Scatter(at, gc, g1, gx, g2, gg, g3, gb, g_send, g_recv)
     acc[...] = jnp.zeros_like(acc)
     for slot in range(4):
         delta[slot] = jnp.sum(do_ref[slot].astype(f32).T * ot_ref[slot], axis=0, keepdims=True)
     ready()
-    for k in range(2):
-        down.a_copy(k).start()
-        up.x_copy(k).start()
-
-    def unit(slot, t, buf, first, slabs, blocks, allowed):
-        size = slabs * blocks * per
-        pick = (slice(first, first + slabs), slice(0, blocks))
-        keys = kv_ref[(0,) + pick + (t,)].reshape(size, HEAD_DIM)
-        values = kv_ref[(1,) + pick + (t,)].reshape(size, HEAD_DIM)
-        query = q_ref[slot]
-        d_out = do_ref[slot]
-        scores = nt(keys, query) * LOG_SCALE - ls_ref[slot]
-        if allowed is not None:
-            scores = jnp.where(allowed, scores, NEGATIVE)
-        prob = jnp.exp2(scores)
-        d_probs = nt(values, d_out)
-        d_scores = (prob * (d_probs - delta[slot])).astype(bf16)
-        shape = (slabs, blocks, per, HEAD_DIM)
-        grads[(buf, 1) + pick] += nn(prob.astype(bf16), d_out).reshape(shape)
-        grads[(buf, 0) + pick] += nn(d_scores, query).reshape(shape)
-        acc[slot] += tn(keys, d_scores)
-
-    def d_copy(slot):
-        return remote(
-            dqs.at[slot], dq_ref.at[slab], d_send.at[slot], d_recv.at[slab],
-            at.dev(slot, at.turned(slot)),
-        )
-
-    def slot_step(slot, t, buf):
-        if slot > 0:
-            unit(slot, t, buf, 0, slot, 4, None)
-        mine = at.turned(slot)
-        for blocks, chosen in ((2, mine < 2), (4, mine >= 2)):
-
-            @pl.when(chosen)
-            def _():
-                allowed = attend_mask(blocks * per, rows, per, t, mine)
-                unit(slot, t, buf, slot, 1, blocks, allowed)
-
-        @pl.when(t == STEPS - 1)
-        def _():
-            dqs[slot] = (acc[slot] * HEAD_SCALE).T.astype(bf16)
-            home = jnp.logical_and(slab == slot, even)
-
-            @pl.when(home)
-            def _():
-                dq_ref[slab] = dqs[slot]
-
-            @pl.when(jnp.logical_not(home))
-            def _():
-                d_copy(slot).start()
-
-    def part(buf, x, c):
-        return grads[buf, :, :, 2 * x + c]
-
-    def near_copy(t):
-        return remote(
-            near_out.at[t], near_in.at[t], n_send.at[t], n_recv.at[t], at.dev(slab, at.core_seat)
-        )
-
-    def wide_copy(t):
-        return remote(
-            wide_out.at[t], wide_in.at[t], w_send.at[t], w_recv.at[t], at.dev(slab, at.x_seat)
-        )
-
-    def home_copy(t, k):
-        return remote(
-            home_out.at[t, :, k], dkv_ref.at[slab, :, t], h_send.at[t, k], h_recv.at[t, slab],
-            at.dev(k, seat),
-        )
-
-    def near_stage(t, buf):
-        near_copy(t).wait_recv()
-        wide_out[t] = (part(buf, 1 - wide, core) + near_in[t, 1 - wide].astype(f32)).astype(bf16)
-        wide_copy(t).start()
-        kept[...] = part(buf, wide, core) + near_in[t, wide].astype(f32)
-
-    def wide_stage(t):
-        wide_copy(t).wait_recv()
-        home_out[t, 0] = ((kept[0] + wide_in[t, 0].astype(f32)) * HEAD_SCALE).astype(bf16)
-        home_out[t, 1] = (kept[1] + wide_in[t, 1].astype(f32)).astype(bf16)
-        dkv_ref[slab, :, t] = home_out[t, :, slab]
-        for step in range(1, 4):
-            home_copy(t, lax.rem(slab + step, 4)).start()
-
-    def go(t, _):
-        buf = lax.rem(t, 2)
-        grads[buf] = jnp.zeros_like(grads[buf])
-        slot_step(3, t, buf)
-
-        @pl.when(t > 0)
-        def _():
-            near_stage(t - 1, 1 - buf)
-
-        slot_step(0, t, buf)
-        slot_step(2, t, buf)
-
-        @pl.when(t > 0)
-        def _():
-            wide_stage(t - 1)
-
-        slot_step(1, t, buf)
-        for x in range(2):
-            near_out[t, x] = part(buf, x, 1 - core).astype(bf16)
-        near_copy(t).start()
-        for k in range(2):
-
-            @pl.when(t == k + 1)
-            def _():
-                down.a_add(k)
-                down.b_copy(k).start()
-
-        return 0
-
-    lax.fori_loop(0, STEPS, go, 0)
-    near_stage(STEPS - 1, (STEPS - 1) % 2)
-    half = gd_ref.shape[0] // 2
-    for k in range(2):
-        up.x_add(k)
-        gd_ref[k * half : (k + 1) * half, :] = down.b_add(k).T
-    wide_stage(STEPS - 1)
-    for k in range(2):
-        down.a_copy(k).wait_send()
-        down.b_copy(k).wait_send()
-        up.x_copy(k).wait_send()
-
-    def finish(t, _):
-        near_copy(t).wait_send()
-        wide_copy(t).wait_send()
-        for step in range(1, 4):
-            k = lax.rem(slab + step, 4)
-            home_copy(t, k).wait_send()
-            slot = dkv_ref.at[k, :, t]
-            remote(slot, slot, h_send.at[t, k], h_recv.at[t, k], at.dev(k, seat)).wait_recv()
-        return 0
-
-    lax.fori_loop(0, STEPS, finish, 0)
-    for k in range(4):
-        home = jnp.logical_and(slab == k, even)
-
-        @pl.when(jnp.logical_not(home))
-        def _():
-            d_copy(k).wait_send()
-            slot = dq_ref.at[k]
-            remote(slot, slot, d_send.at[k], d_recv.at[k], at.dev(k, seat)).wait_recv()
-
-
-def tail_kernel(
-    dq_ref, dkv_ref, n_one_ref, wq_ref, wk_ref, wv_ref, x_ref, gain_ref, dh_ref, vec_ref, go_ref,
-    cnt_ref, up_ref,
-    ig_ref, gq_ref, gk_ref, gv_ref, go_out, gu_ref, g1_ref, b1_ref, g2_ref, b2_ref, loss_ref,
-    vsum_ref,
-    ga, rc, s1, rx, s2, ra, s3, rb, g_send, g_recv, ua, u3, ub, u_send, u_recv, bs, br, dcat,
-    b_send, b_recv,
-    tile, core_in, x_buf, x_in, z_buf, z_in, t_send, t_recv,
-):
-    at = Place()
-    rows = x_ref.shape[0]
-    part_rows = rows // CHUNKS
-    ready = greet(at.peers(True, False, True, True))
-    scatter = Scatter(at, rc, s1, rx, s2, ra, s3, rb, g_send, g_recv)
-    up = Scatter(at, None, None, None, up_ref, ua, u3, ub, u_send, u_recv)
+    own.c_copy(0, go_ref).start()
+    first.a_copy(0).start()
+    rest.x_copy(0).start()
 
     def b_copy(c):
         return remote(bs.at[c], br.at[c], b_send.at[c], b_recv.at[c], at.other_side())
 
-    dcat[0] = heads_row(dq_ref, slice(None))
-    for j in range(2):
-        dcat[1 + j] = jnp.concatenate([dkv_ref[h, j] for h in range(4)], axis=1)
-    ready()
-    scatter.c_copy(0, go_ref).start()
-    for k in range(2):
-        up.a_copy(k).start()
-
-    def side_part(c, _):
-        part = pl.ds(pl.multiple_of(c * part_rows, part_rows), part_rows)
-        bs[c] = (
-            nt(dcat[0, part, :], wq_ref[...])
-            + nt(dcat[1, part, :], wk_ref[...])
-            + nt(dcat[2, part, :], wv_ref[...])
-        ).astype(bf16)
-        b_copy(c).start()
-        return 0
-
-    lax.fori_loop(0, CHUNKS, side_part, 0)
-    scatter.core_add(0, go_ref)
-    scatter.x_copy(0).start()
-    for j in range(3):
-        ga[j] = tn(n_one_ref[...], dcat[j]).astype(bf16).reshape(ga.shape[1:])
-        scatter.c_copy(j + 1, ga.at[j]).start()
-        if j > 0:
-            scatter.core_add(j, ga.at[j - 1])
-            scatter.x_copy(j).start()
-    scatter.core_add(3, ga.at[2])
-    scatter.x_copy(3).start()
-    for k in range(2):
-        up.a_add(k)
-        up.b_copy(k).start()
-    tile[...] = vec_ref[...]
-    tile[3:5, :] = jnp.zeros_like(tile[3:5, :])
-    scatter.x_add(0)
-    scatter.a_copy(0).start()
-
-    def side_sum(c, _):
-        part = pl.ds(pl.multiple_of(c * part_rows, part_rows), part_rows)
-        b_copy(c).wait()
-        d_one = bs[c].astype(f32) + br[c].astype(f32)
-        normed, inverse = norm_stats(x_ref[part, :])
-        scaled = d_one * gain_ref[...]
-        first = jnp.mean(scaled, axis=-1, keepdims=True)
-        second = jnp.mean(scaled * normed, axis=-1, keepdims=True)
-        ig_ref[part, :] = dh_ref[part, :] + inverse * (scaled - first - normed * second)
-        tile[3:4, :] += jnp.sum(d_one * normed, axis=0, keepdims=True)
-        tile[4:5, :] += jnp.sum(d_one, axis=0, keepdims=True)
-        for k in range(1, 4):
-
-            @pl.when(c == k)
-            def _():
-                scatter.x_add(k)
-                scatter.a_copy(k).start()
-                scatter.a_add(k - 1)
-                scatter.b_copy(k - 1).start()
-
-        return 0
-
-    lax.fori_loop(0, CHUNKS, side_sum, 0)
-    total = Summed(at, tile, core_in, x_buf, x_in, z_buf, z_in, t_send, t_recv)
-    total.one()
-    half = gu_ref.shape[1] // 2
-    for k in range(2):
-        gu_ref[:, k * half : (k + 1) * half] = up.b_add(k)
-    total.two()
-    scatter.a_add(3)
-    scatter.b_copy(3).start()
-    go_out[...] = scatter.b_add(0).T
-    total.three()
-    gq_ref[...] = scatter.b_add(1)
-    gk_ref[...] = scatter.b_add(2)
-    gv_ref[...] = scatter.b_add(3)
-    vsum_ref[...] = total.four()
-    share = gq_ref.shape[0]
-    for k in range(SEQ_DEV):
-
-        @pl.when(at.pos == k)
-        def _():
-            for line, ref in ((3, g1_ref), (4, b1_ref), (0, g2_ref), (1, b2_ref)):
-                ref[...] = vsum_ref[line : line + 1, k * share : (k + 1) * share]
-
-    loss_ref[...] = jnp.sum(vsum_ref[2:3, :], axis=1, keepdims=True) / (2.0 * cnt_ref[0:1, 0:1])
-    for k in range(4):
-        scatter.c_copy(k, go_ref if k == 0 else ga.at[k - 1]).wait_send()
-        scatter.x_copy(k).wait_send()
-        scatter.a_copy(k).wait_send()
-        scatter.b_copy(k).wait_send()
-    for k in range(2):
-        up.a_copy(k).wait_send()
-        up.b_copy(k).wait_send()
+    def attention(grads, kept):
+        def unit(slot, t, buf, start, slabs, blocks, allowed):
+            size = slabs * blocks * per
+            pick = (slice(start, start + slabs), slice(0, blocks))
+            keys = kv_ref[(0,) + pick + (t,)].reshape(size, HEAD_DIM)
+            values = kv_ref[(1,) + pick + (t,)].reshape(size, HEAD_DIM)
+            query = q_ref[slot]
+            d_out = do_ref[slot]
+            scores = nt(keys, query) * LOG_SCALE - ls_ref[slot]
+            if allowed is not None:
+                scores = jnp.where(allowed, scores, NEGATIVE)
+            prob = jnp.exp2(scores)
+            d_probs = nt(values, d_out)
+            d_scores = (prob * (d_probs - delta[slot])).astype(bf16)
+            shape = (slabs, blocks, per, HEAD_DIM)
+            grads[(buf, 1) + pick] += nn(prob.astype(bf16), d_out).reshape(shape)
+            grads[(buf, 0) + pick] += nn(d_scores, query).reshape(shape)
+            acc[slot] += tn(keys, d_scores)
+
+        def d_copy(slot):
+            return remote(
+                dqs.at[slot], dq_ref.at[slab], d_send.at[slot], d_recv.at[slab],
+                at.dev(slot, at.turned(slot)),
+            )
+
+        def slot_step(slot, t, buf):
+            if slot > 0:
+                unit(slot, t, buf, 0, slot, 4, None)
+            mine = at.turned(slot)
+            for blocks, chosen in ((2, mine < 2), (4, mine >= 2)):
+
+                @pl.when(chosen)
+                def _():
+                    allowed = attend_mask(blocks * per, rows, per, t, mine)
+                    unit(slot, t, buf, slot, 1, blocks, allowed)
+
+            @pl.when(t == STEPS - 1)
+            def _():
+                dqs[slot] = (acc[slot] * HEAD_SCALE).T.astype(bf16)
+                home = jnp.logical_and(slab == slot, even)
+
+                @pl.when(home)
+                def _():
+                    dq_ref[slab] = dqs[slot]
+
+                @pl.when(jnp.logical_not(home))
+                def _():
+                    d_copy(slot).start()
+
+        def part(buf, x, c):
+            return grads[buf, :, :, 2 * x + c]
+
+        def near_copy(t):
+            return remote(
+                near_out.at[lax.rem(t, 2)], near_in.at[lax.rem(t, 2)], n_send.at[t], n_recv.at[t], at.dev(slab, at.core_seat)
+            )
+
+        def wide_copy(t):
+            return remote(
+                wide_out.at[t], wide_in.at[t], w_send.at[t], w_recv.at[t], at.dev(slab, at.x_seat)
+            )
+
+        def home_copy(t, k):
+            return remote(
+                home_out.at[t, :, k], dkv_ref.at[slab, :, t], h_send.at[t, k], h_recv.at[t, slab],
+                at.dev(k, seat),
+            )
+
+        def near_stage(t, buf):
+            near_copy(t).wait_recv()
+            wide_out[t] = (part(buf, 1 - wide, core) + near_in[buf, 1 - wide].astype(f32)).astype(bf16)
+            wide_copy(t).start()
+            kept[buf] = part(buf, wide, core) + near_in[buf, wide].astype(f32)
+
+        def wide_stage(t, buf):
+            wide_copy(t).wait_recv()
+            home_out[t, 0] = ((kept[buf, 0] + wide_in[t, 0].astype(f32)) * HEAD_SCALE).astype(bf16)
+            home_out[t, 1] = (kept[buf, 1] + wide_in[t, 1].astype(f32)).astype(bf16)
+            dkv_ref[slab, :, t] = home_out[t, :, slab]
+            for step in range(1, 4):
+                home_copy(t, lax.rem(slab + step, 4)).start()
+
+        def go(t, _):
+            buf = lax.rem(t, 2)
+            grads[buf] = jnp.zeros_like(grads[buf])
+            slot_step(3, t, buf)
+
+            @pl.when(t > 1)
+            def _():
+                wide_stage(t - 2, buf)
+
+            @pl.when(t > 0)
+            def _():
+                near_stage(t - 1, 1 - buf)
+
+            slot_step(0, t, buf)
+
+            @pl.when(t == 0)
+            def _():
+                own.core_add(0, go_ref)
+                own.x_copy(0).start()
+
+            @pl.when(t == 1)
+            def _():
+                first.a_add(0)
+                first.b_copy(0).start()
+
+            @pl.when(t == 2)
+            def _():
+                rest.x_add(0)
+                rest.a_copy(0).start()
+
+            @pl.when(t == 3)
+            def _():
+                own.x_add(0)
+                own.a_copy(0).start()
+
+            slot_step(2, t, buf)
+            slot_step(1, t, buf)
+
+            @pl.when(t > 1)
+            def _():
+                near_copy(t - 2).wait_send()
+
+            for x in range(2):
+                near_out[buf, x] = part(buf, x, 1 - core).astype(bf16)
+            near_copy(t).start()
+            return 0
+
+        lax.fori_loop(0, STEPS, go, 0)
+        wide_stage(STEPS - 2, STEPS % 2)
+        near_stage(STEPS - 1, (STEPS - 1) % 2)
+        rest.x_copy(1).start()
+        rest.x_copy(2).start()
+        rest.a_add(0)
+        rest.b_copy(0).start()
+        own.a_add(0)
+        own.b_copy(0).start()
+        gd_ref[:, : gd_ref.shape[1] // 2] = first.b_add(0)
+        wide_stage(STEPS - 1, (STEPS - 1) % 2)
+
+        def finish(t, _):
+            wide_copy(t).wait_send()
+            for step in range(1, 4):
+                k = lax.rem(slab + step, 4)
+                home_copy(t, k).wait_send()
+                slot = dkv_ref.at[k, :, t]
+                remote(slot, slot, h_send.at[t, k], h_recv.at[t, k], at.dev(k, seat)).wait_recv()
+            return 0
+
+        lax.fori_loop(0, STEPS, finish, 0)
+        near_copy(STEPS - 2).wait_send()
+        near_copy(STEPS - 1).wait_send()
+        for k in range(4):
+            home = jnp.logical_and(slab == k, even)
+
+            @pl.when(jnp.logical_not(home))
+            def _():
+                d_copy(k).wait_send()
+                slot = dq_ref.at[k]
+                remote(slot, slot, d_send.at[k], d_recv.at[k], at.dev(k, seat)).wait_recv()
+
+    pl.run_scoped(
+        attention,
+        pltpu.VMEM((2, 2, 4, 4, per, HEAD_DIM), f32),
+        pltpu.VMEM((2, 2, 4, per, HEAD_DIM), f32),
+    )
+
+    def ending(n_one, wq, wk, wv, x, dh, dcat, ga):
+        loads = [
+            pltpu.make_async_copy(src, dst, load.at[k])
+            for k, (src, dst) in enumerate(
+                (
+                    (wq_hbm, wq), (wk_hbm, wk), (wv_hbm, wv), (n_one_hbm, n_one), (x_hbm, x),
+                    (dh_hbm, dh),
+                )
+            )
+        ]
+        for copy in loads:
+            copy.start()
+        dcat[0] = heads_row(dq_ref, slice(None))
+        for j in range(2):
+            dcat[1 + j] = jnp.concatenate(
+                [dkv_ref[h, j].reshape(rows, HEAD_DIM) for h in range(4)], axis=1
+            )
+        for k in range(3):
+            loads[k].wait()
+
+        def side_part(c, _):
+            part = pl.ds(pl.multiple_of(c * part_rows, part_rows), part_rows)
+            bs[c] = (
+                nt(dcat[0, part, :], wq[...])
+                + nt(dcat[1, part, :], wk[...])
+                + nt(dcat[2, part, :], wv[...])
+            ).astype(bf16)
+            b_copy(c).start()
+            return 0
+
+        lax.fori_loop(0, CHUNKS, side_part, 0)
+        loads[3].wait()
+        for j in range(3):
+            ga[j] = tn(n_one[...], dcat[j]).astype(bf16).reshape(ga.shape[1:])
+            own.c_copy(j + 1, ga.at[j]).start()
+            if j > 0:
+                own.core_add(j, ga.at[j - 1])
+                own.x_copy(j).start()
+        own.core_add(3, ga.at[2])
+        own.x_copy(3).start()
+        for k in range(1, 3):
+            rest.x_add(k)
+            rest.a_copy(k).start()
+        tile[...] = vec_ref[...]
+        tile[3:5, :] = jnp.zeros_like(tile[3:5, :])
+        loads[4].wait()
+        loads[5].wait()
+
+        def side_sum(c, _):
+            part = pl.ds(pl.multiple_of(c * part_rows, part_rows), part_rows)
+            b_copy(c).wait()
+            d_one = bs[c].astype(f32) + br[c].astype(f32)
+            normed, inverse = norm_stats(x[part, :])
+            scaled = d_one * gain_ref[...]
+            first_mean = jnp.mean(scaled, axis=-1, keepdims=True)
+            second_mean = jnp.mean(scaled * normed, axis=-1, keepdims=True)
+            ig_ref[part, :] = dh[part, :] + inverse * (scaled - first_mean - normed * second_mean)
+            tile[3:4, :] += jnp.sum(d_one * normed, axis=0, keepdims=True)
+            tile[4:5, :] += jnp.sum(d_one, axis=0, keepdims=True)
+            for k in range(1, 4):
+
+                @pl.when(c == k * CHUNKS // 4)
+                def _():
+                    own.x_add(k)
+                    own.a_copy(k).start()
+                    if k < 3:
+                        rest.a_add(k)
+                        rest.b_copy(k).start()
+                    if k > 1:
+                        own.a_add(k - 1)
+                        own.b_copy(k - 1).start()
+
+            return 0
+
+        lax.fori_loop(0, CHUNKS, side_sum, 0)
+        total = Summed(at, tile, core_in, x_buf, x_in, z_buf, z_in, t_send, t_recv)
+        total.one()
+        half = gu_ref.shape[1] // 2
+        gd_ref[:, half:] = rest.b_add(0)
+        total.two()
+        for k in range(2):
+            gu_ref[:, k * half : (k + 1) * half] = rest.b_add(1 + k)
+        go_out[...] = own.b_add(0)
+        own.a_add(3)
+        own.b_copy(3).start()
+        total.three()
+        gq_ref[...] = own.b_add(1)
+        gk_ref[...] = own.b_add(2)
+        gv_ref[...] = own.b_add(3)
+        vsum_ref[...] = total.four()
+        share = gq_ref.shape[0]
+        for k in range(SEQ_DEV):
+
+            @pl.when(at.pos == k)
+            def _():
+                for line, ref in ((3, g1_ref), (4, b1_ref), (0, g2_ref), (1, b2_ref)):
+                    ref[...] = vsum_ref[line : line + 1, k * share : (k + 1) * share]
+
+        loss_ref[...] = jnp.sum(vsum_ref[2:3, :], axis=1, keepdims=True) / (
+            2.0 * cnt_ref[0:1, 0:1]
+        )
+        for k in range(4):
+            own.c_copy(k, go_ref if k == 0 else ga.at[k - 1]).wait_send()
+            own.x_copy(k).wait_send()
+            own.a_copy(k).wait_send()
+            own.b_copy(k).wait_send()
+        for k in range(3):
+            rest.x_copy(k).wait_send()
+            rest.a_copy(k).wait_send()
+            rest.b_copy(k).wait_send()
+        first.a_copy(0).wait_send()
+        first.b_copy(0).wait_send()
+
+    width, local = wq_hbm.shape
+    pl.run_scoped(
+        ending,
+        pltpu.VMEM((rows, width), bf16),
+        pltpu.VMEM((width, local), bf16),
+        pltpu.VMEM((width, local), bf16),
+        pltpu.VMEM((width, local), bf16),
+        pltpu.VMEM((rows, width), f32),
+        pltpu.VMEM((rows, width), f32),
+        pltpu.VMEM((3, rows, local), bf16),
+        pltpu.VMEM((3,) + go_ref.shape, bf16),
+    )
+
+
+def copy_kernel(count, *refs):
+    ins, outs, held, load, store = (
+        refs[:count], refs[count : 2 * count], refs[2 * count : 3 * count], refs[-2], refs[-1],
+    )
+    loads = [pltpu.make_async_copy(a, h, load.at[k]) for k, (a, h) in enumerate(zip(ins, held))]
+    stores = [pltpu.make_async_copy(h, o, store.at[k]) for k, (h, o) in enumerate(zip(held, outs))]
+    for copy in loads:
+        copy.start()
+    for one, two in zip(loads, stores):
+        one.wait()
+        two.start()
+    for copy in stores:
+        copy.wait()
 
 
 def in_vmem():
@@ -967,29 +1043,30 @@
     step_rows = rows // STEPS
     part_rows = rows // CHUNKS
 
-    n_one, kv_all, q_all, o_t, log_sum, ctx, count, wo_in = call(
+    n_one, kv_all, q_all, o_t, log_sum, ctx, ctx_in, count, wo_in = call(
         forward_kernel, "forward", 1,
         (
             out((rows, width), bf16),
-            out((2, 4, 4, STEPS, step_rows, HEAD_DIM), bf16),
+            out((2, 4, 4, FSTEPS, rows // FSTEPS, HEAD_DIM), bf16),
             out((4, rows, HEAD_DIM), bf16),
             out((4, HEAD_DIM, rows), f32),
             out((4, 1, rows), f32),
+            out((heads, rows, HEAD_DIM), bf16),
             out((heads, rows, HEAD_DIM), bf16),
             out((8, 128), f32),
             out((local, width), bf16),
         ),
         [in_vmem()] * 8,
         [
-            pltpu.VMEM((heads, 2, STEPS, step_rows, HEAD_DIM), bf16),
+            pltpu.VMEM((heads, 2, FSTEPS, rows // FSTEPS, HEAD_DIM), bf16),
             pltpu.VMEM((heads, rows, HEAD_DIM), bf16),
             pltpu.VMEM((4, rows, HEAD_DIM), bf16),
             pltpu.VMEM((4, 1, rows), f32),
             pltpu.VMEM((4, 1, rows), f32),
-            dma(STEPS, 4), dma(STEPS, 4), dma(4), dma(4),
+            dma(FSTEPS, 4), dma(FSTEPS, 4), dma(4), dma(4),
         ]
-        + [dma(STEPS)] * 6
-        + [dma(4)] * 2
+        + [dma(FSTEPS)] * 6
+        + [dma(4)] * 4
         + [dma(2)]
         + summed_scratch((8, 128)),
         (
@@ -1002,20 +1079,20 @@
     share = width // SEQ_DEV
     split = (4, 2, 2, share)
     piece = hidden_units // 2
-    output, d_hidden, do_all, up_part, down_part, grad_out_t, vectors = call(
+    output, d_hidden, do_all, part_one, part_two, grad_out_t, vectors = call(
         functools.partial(middle_kernel, float(rows * dp_size)), "middle", 2,
         (
             out((rows, width), f32),
             out((rows, width), f32),
             out((4, rows, HEAD_DIM), bf16),
-            out((2, 4, 2, share, piece), bf16),
-            out((2, 2, 2, share, piece), bf16),
+            out((3, 4, 2, share, piece), bf16),
+            out((1, 2, 2, share, piece), bf16),
             out((width, local), bf16),
             out((8, width), f32),
         ),
         [
-            in_vmem(), in_hbm(), in_hbm(), in_hbm(), in_vmem(), in_vmem(), in_hbm(), in_hbm(),
-            in_hbm(), in_vmem(), in_vmem(),
+            in_vmem(), in_vmem(), in_hbm(), in_hbm(), in_hbm(), in_vmem(), in_vmem(), in_hbm(),
+            in_hbm(), in_hbm(), in_vmem(), in_vmem(),
         ],
         [
             pltpu.VMEM((rows, width), f32),
@@ -1025,7 +1102,6 @@
             pltpu.VMEM((hidden_units, width), bf16),
             pltpu.VMEM((rows, width), f32),
             dma(6),
-            pltpu.VMEM((heads, rows, HEAD_DIM), bf16),
             pltpu.VMEM((rows, width), f32),
             pltpu.VMEM((rows, 1), f32),
             pltpu.VMEM((rows, width), bf16),
@@ -1036,63 +1112,54 @@
             pltpu.VMEM((heads, rows, HEAD_DIM), bf16),
         ]
         + [pltpu.VMEM((CHUNKS, part_rows, width), bf16)] * 4
-        + [dma(CHUNKS)] * 6
+        + [dma(CHUNKS)] * 4
         + [dma(CHUNKS, 4)] * 2
         + [
             pltpu.VMEM((2,) + split + (piece,), bf16),
             pltpu.VMEM((4, 4, 2, share, piece), bf16),
             pltpu.VMEM((4, 4, 2, share, piece), bf16),
-            pltpu.VMEM((2, 4, share, piece), bf16),
+            pltpu.VMEM((1, 4, share, piece), bf16),
             dma(2, 4), dma(2, 4),
         ],
         (
-            ctx, inputs, w_out, wo_in, row(ln2_gain), row(ln2_bias), w_up, w_down, teacher,
+            ctx, ctx_in, inputs, w_out, wo_in, row(ln2_gain), row(ln2_bias), w_up, w_down, teacher,
             valid_mask.astype(f32).reshape(rows, 1), count,
         ),
     )
-    d_query, d_kv, grad_down, up_part = call(
+    (
+        input_grad, grad_query, grad_key, grad_value, grad_out_t, grad_up, grad_down_t, gain_one,
+        bias_one, gain_two, bias_two, loss, sums,
+    ) = call(
         backward_kernel, "backward", 3,
-        (
-            out((heads, rows, HEAD_DIM), bf16),
-            out((heads, 2, STEPS, step_rows, HEAD_DIM), bf16),
-            out((hidden_units, share), f32),
-            out((2, 2, 2, share, piece), bf16),
-        ),
-        [in_vmem()] * 7,
+        (out((rows, width), f32),)
+        + (out((share, local), f32),) * 4
+        + (out((share, hidden_units), f32),) * 2
+        + (out((1, share), f32),) * 4
+        + (out((1, 1), f32), out((8, width), f32)),
+        [in_vmem()] * 8 + [in_hbm()] * 6 + [in_vmem()] * 3,
         [
-            pltpu.VMEM((2, 2, 4, 4, step_rows, HEAD_DIM), f32),
+            pltpu.VMEM((heads, rows, HEAD_DIM), bf16),
+            pltpu.VMEM((heads, 2, STEPS, step_rows, HEAD_DIM), bf16),
             pltpu.VMEM((4, HEAD_DIM, rows), f32),
             pltpu.VMEM((4, 1, rows), f32),
-            pltpu.VMEM((STEPS, 2, 2, 4, step_rows, HEAD_DIM), bf16),
-            pltpu.VMEM((STEPS, 2, 2, 4, step_rows, HEAD_DIM), bf16),
+            pltpu.VMEM((2, 2, 2, 4, step_rows, HEAD_DIM), bf16),
+            pltpu.VMEM((2, 2, 2, 4, step_rows, HEAD_DIM), bf16),
             pltpu.VMEM((STEPS, 2, 4, step_rows, HEAD_DIM), bf16),
             pltpu.VMEM((STEPS, 2, 4, step_rows, HEAD_DIM), bf16),
             pltpu.VMEM((STEPS, 2, 4, step_rows, HEAD_DIM), bf16),
             pltpu.VMEM((4, rows, HEAD_DIM), bf16),
-            pltpu.VMEM((2, 4, step_rows, HEAD_DIM), f32),
             dma(STEPS), dma(STEPS), dma(STEPS), dma(STEPS), dma(STEPS, 4), dma(STEPS, 4),
             dma(4), dma(4),
-            pltpu.VMEM((2, 4, share, piece), bf16),
-            pltpu.VMEM((2, 2, share, piece), bf16),
-            pltpu.VMEM((2, 2, share, piece), bf16),
-            pltpu.VMEM((2, share, piece), bf16),
-            dma(4, 2), dma(4, 2), dma(4, 2), dma(4, 2),
-        ],
-        (kv_all, q_all, o_t, log_sum, do_all, up_part, down_part),
-    )
-    (
-        input_grad, grad_query, grad_key, grad_value, grad_out, grad_up, gain_one, bias_one,
-        gain_two, bias_two, loss, sums,
-    ) = call(
-        tail_kernel, "tail", 4,
-        (out((rows, width), f32),)
-        + (out((share, local), f32),) * 3
-        + (out((local, share), f32), out((share, hidden_units), f32))
-        + (out((1, share), f32),) * 4
-        + (out((1, 1), f32), out((8, width), f32)),
-        [in_vmem()] * 13,
-        [
-            pltpu.VMEM((3,) + split + (local,), bf16),
+            pltpu.VMEM((1, 2, share, piece), bf16),
+            pltpu.VMEM((1, 2, share, piece), bf16),
+            pltpu.VMEM((1, share, piece), bf16),
+            dma(4, 1), dma(4, 1),
+            pltpu.VMEM((3, 4, share, piece), bf16),
+            pltpu.VMEM((3, 2, 2, share, piece), bf16),
+            pltpu.VMEM((3, 2, share, piece), bf16),
+            pltpu.VMEM((3, 2, share, piece), bf16),
+            pltpu.VMEM((3, share, piece), bf16),
+            dma(4, 3), dma(4, 3),
             pltpu.VMEM((4, 4, 2, share, local), bf16),
             pltpu.VMEM((4, 4, 2, share, local), bf16),
             pltpu.VMEM((4, 4, share, local), bf16),
@@ -1101,22 +1168,35 @@
             pltpu.VMEM((4, 2, share, local), bf16),
             pltpu.VMEM((4, share, local), bf16),
             dma(4, 4), dma(4, 4),
-            pltpu.VMEM((2, 2, share, piece), bf16),
-            pltpu.VMEM((2, 2, share, piece), bf16),
-            pltpu.VMEM((2, share, piece), bf16),
-            dma(4, 2), dma(4, 2),
             pltpu.VMEM((CHUNKS, part_rows, width), bf16),
             pltpu.VMEM((CHUNKS, part_rows, width), bf16),
-            pltpu.VMEM((3, rows, local), bf16),
-            dma(CHUNKS), dma(CHUNKS),
+            dma(CHUNKS), dma(CHUNKS), dma(6),
         ]
         + summed_scratch((8, width)),
         (
-            d_query, d_kv.reshape(heads, 2, rows, HEAD_DIM), n_one, w_query, w_key, w_value,
-            inputs, row(ln1_gain), d_hidden, vectors, grad_out_t.reshape(split + (local,)), count,
-            up_part,
+            kv_all.reshape(2, 4, 4, STEPS, step_rows, HEAD_DIM), q_all, o_t, log_sum, do_all,
+            part_one, part_two, grad_out_t.reshape(split + (local,)), n_one, w_query, w_key,
+            w_value, inputs, d_hidden, row(ln1_gain), vectors, count,
         ),
     )
+    if single:
+        leaving = (
+            output, input_grad, grad_query, grad_key, grad_value, grad_out_t, grad_up, grad_down_t,
+            gain_one, bias_one, gain_two, bias_two, loss,
+        )
+        (
+            output, input_grad, grad_query, grad_key, grad_value, grad_out_t, grad_up, grad_down_t,
+            gain_one, bias_one, gain_two, bias_two, loss,
+        ) = pl.pallas_call(
+            functools.partial(copy_kernel, len(leaving)),
+            name="leave",
+            out_shape=tuple(out(array.shape, array.dtype) for array in leaving),
+            in_specs=[in_hbm()] * len(leaving),
+            out_specs=tuple(in_hbm() for _ in leaving),
+            scratch_shapes=[pltpu.VMEM(array.shape, array.dtype) for array in leaving]
+            + [dma(len(leaving)), dma(len(leaving))],
+        )(*leaving)
+    grad_down, grad_out = grad_down_t.T, grad_out_t.T
     small = [gain_one, bias_one, gain_two, bias_two]
     small = [vector.reshape(share) for vector in small]
     loss_value = loss.reshape(())

time: 318 us -> 293 us (0.921)
  local copies, waits for them, and re-layouts: 13.2 us -> 0.86 us
  Pallas kernels: 301 us -> 291 us
    pallas_call x4 -> x3, Pallas kernels: 301 us -> 287 us  [call(): pl.pallas_call(kernel, name=name, out_shape=outs, in_specs=ins, out_specs...]
    unnamed x32 -> x2, local copies, waits for them, and re-layouts: 12.3 us -> 0.01 us
    pallas_call x0 -> x1, Pallas kernels: none -> 4.95 us  [per_device(): pl.pallas_call(functools.partial(copy_kernel, len(leaving)), name='leave'...]
where the time goes in v3:
time: 293 us
  Pallas kernels  291 us (99%)
    pallas_call x3, Pallas kernels, call(): pl.pallas_call(kernel, name=name, out_shape=outs, in_specs=ins, out_specs...  287 us

profile of v3, /device:TPU:0, one launch (start us, length us, event | category | flops | bytes accessed | tf_op | source)
XLA Modules:
  0.0 293.3 jit_solution(12556578978157655580)
XLA Ops:
  0.6 0.0 copy-start
  0.7 86.6 %forward.1 = (bf16[512,1024]{1,0:T(8,128)(2,1)}, bf16[2,4,4,4,128,128]{5,4,3,2,1,0:T(8,128)(2,1)}, bf16[4,512,128]{2,1,0:T(8,128)(2,1)}, f32[4,128,512]{2,1,0:T(...) custom-call(f32[512,1024]{1,0:T(8,128)} %x_hbm.3, ...), custom_call_target="tpu_custom_call" | custom-call | bytes 16777216 | tf_op jit(solution)/shard_map/forward/pallas_call | solution.py:1016
  87.3 0.0 copy-done
  87.3 0.9 copy.26.mask_ref
  88.2 70.7 %middle.1 = (f32[512,1024]{1,0:T(8,128)}, f32[512,1024]{1,0:T(8,128)}, bf16[4,512,128]{2,1,0:T(8,128)(2,1)}, bf16[3,4,2,64,1024]{4,3,2,1,0:T(8,128)(2,1)}, bf16[...) custom-call(bf16[4,512,128]{2,1,0:T(8,128)(2,1)} %get-tuple-element.54.ctx_ref, ...), custom_call_target="tpu_custom_call" | custom-call | bytes 16777216 | tf_op jit(solution)/shard_map/middle/pallas_call | solution.py:1016
  158.9 129.2 %backward.1 = (f32[512,1024]{1,0:T(8,128)}, f32[64,512]{1,0:T(8,128)}, f32[64,512]{1,0:T(8,128)}, f32[64,512]{1,0:T(8,128)}, f32[64,512]{1,0:T(8,128)}, /*index=...) custom-call(bf16[2,4,4,4,128,128]{5,4,3,2,1,0:T(8,128)(2,1)} %get-tu, ...), custom_call_target="tpu_custom_call" | custom-call | bytes 16777216 | tf_op jit(solution)/shard_map/backward/pallas_call | solution.py:1016
  288.1 5.0 %leave.1 = (f32[512,1024]{1,0:T(8,128)}, f32[512,1024]{1,0:T(8,128)}, f32[64,512]{1,0:T(8,128)}, f32[64,512]{1,0:T(8,128)}, f32[64,512]{1,0:T(8,128)}, /*index=5...) custom-call(f32[512,1024]{1,0:T(8,128)} %get-tuple-element.58.refs_0, ...), custom_call_target="tpu_custom_call" | custom-call | tf_op jit(solution)/shard_map/leave/pallas_call | solution.py:1190
  (1 shorter events, 0.0 us)
Async XLA Ops:
  0.6 86.6 %copy-start = (s32[512]{0:T(512)S(1)}, s32[512]{0:T(512)}, u32[]{:S(2)}) copy-start(s32[512]{0:T(512)} %param.25) | copy-start | bytes 6148
